TPU v7x, 256 devices: a whole 4x4x8 slice. The times are simulated.
256 devices in a mesh: subj: 8 (over x, core), space: 32 (over y, z).
Axes of the slice: x: 4, y: 4, z: 8, core: 2. Of those that a mesh axis runs over, the one named last changes fastest.
Arguments:
- images: bfloat16 [16, 2048, 16, 128], P('subj', 'space'), may hold values from -6 to 6
- velocity: float32 [3, 16, 2048, 16, 128], P(None, 'subj', 'space'), may hold values from -4 to 4
- weights: bfloat16 [3, 16, 2048, 16, 128], P(None, 'subj', 'space'), may hold values from 0 to 1
- template: float32 [2048, 16, 128], P('space', 'subj'), may hold values from -6 to 6
- owners: int32 [16, 2048, 1], P('subj', 'space'), may hold values from 0 to 31; in each aligned block of 64 rows (0 to 63, 64 to 127, ..., all dimensions but the last counted through in order) at most 4 rows name the same one
- local_rows: int32 [16, 2048], P('subj', 'space'), may hold values from 0 to 63
- tile_counts: int32 [16, 32], P('subj', 'space'), may hold values from 32 to 64
Outputs:
- new_velocity: float32 [3, 16, 2048, 16, 128], P(None, 'subj', 'space')
- new_template: float32 [2048, 16, 128], P('space', 'subj')
Inputs may be any that keep to these rules, and one draw needn't show every extreme that they name: `owners`: for each subject and each aligned block of 64 tiles, no value appears more than 4 times, and some value appears exactly 4 times.
All inputs are finite; a program needn't handle non-finite values.
Results may differ from a plain program's by a relative error of at most 0.0006.
Values may be sent and summed in bfloat16 or wider, within the bound.
A program may use at most 64 MiB of HBM per device.

v0:
```python
import jax
import jax.numpy as jnp
from jax import lax
from jax.sharding import PartitionSpec as P

BX = 4
BY = 4
ITERS = 2


ridge = 0.25


def extended(block, sides, width):
    for axis, dim in sides:
        count = lax.axis_size(axis)
        forward = [(i, i + 1) for i in range(count - 1)]
        backward = [(target, source) for source, target in forward]
        low = lax.ppermute(
            lax.slice_in_dim(block, block.shape[dim] - width, None, axis=dim), axis, forward
        )
        high = lax.ppermute(lax.slice_in_dim(block, 0, width, axis=dim), axis, backward)
        block = jnp.concatenate([low, block, high], axis=dim)
    return block


def shift_up(field, axis):
    body_part = lax.slice_in_dim(field, 1, field.shape[axis], axis=axis)
    edge = jnp.zeros_like(lax.slice_in_dim(field, 0, 1, axis=axis))
    return jnp.concatenate([body_part, edge], axis)


def shift_down(field, axis):
    body_part = lax.slice_in_dim(field, 0, field.shape[axis] - 1, axis=axis)
    edge = jnp.zeros_like(lax.slice_in_dim(field, 0, 1, axis=axis))
    return jnp.concatenate([edge, body_part], axis)


def trilinear(brick, frac_x, frac_y, frac_z):
    depth = brick.ndim
    total = jnp.zeros_like(brick)
    for offset_x in (0, 1):
        moved_x = brick if offset_x == 0 else shift_up(brick, depth - 3)
        weight_x = 1.0 - frac_x if offset_x == 0 else frac_x
        for offset_y in (0, 1):
            moved = moved_x if offset_y == 0 else shift_up(moved_x, depth - 2)
            weight_y = 1.0 - frac_y if offset_y == 0 else frac_y
            along_z = (1.0 - frac_z) * moved + frac_z * shift_up(moved, depth - 1)
            total = total + weight_x * weight_y * along_z
    return total


def gradients(field):
    depth = field.ndim
    return jnp.stack(
        [
            0.5 * (shift_up(field, depth - 3 + offset) - shift_down(field, depth - 3 + offset))
            for offset in range(3)
        ]
    )


def smooth_z(field):
    depth = field.ndim
    return 0.25 * shift_down(field, depth - 1) + 0.5 * field + 0.25 * shift_up(field, depth - 1)


def predict(warped, grads, field):
    return warped + (grads[0] * field[0] + grads[1] * field[1]) + grads[2] * field[2]


def body(images, velocity, weights, template, owners, local_rows, tile_counts):
    spaces = lax.axis_size("space")
    groups = lax.axis_size("subj")
    subj_dev = images.shape[0]
    rows_dev = images.shape[1]
    plane = images.shape[2]
    depth_z = images.shape[3]
    cap = 2 * rows_dev // spaces
    subjects = subj_dev * groups
    position = jnp.arange(rows_dev, dtype=jnp.int32)[None, :]
    first = tile_counts // 2
    alive = (position < first) | (position >= rows_dev - (tile_counts - first))
    owner = owners[:, :, 0]
    hits = (owner[:, :, None] == jnp.arange(spaces, dtype=jnp.int32)[None, None, :]).astype(
        jnp.int32
    )
    hits = hits * alive.astype(jnp.int32)[:, :, None]
    before = jnp.cumsum(hits, axis=1) - hits
    place = jnp.sum(before * hits, axis=2)
    slot = jnp.where(alive, owner * cap + place, spaces * cap)
    request = jnp.zeros((subj_dev, spaces * cap), jnp.int32)
    request = request.at[jnp.arange(subj_dev)[:, None], slot].set(local_rows, mode="drop")
    request = request.reshape(subj_dev, spaces, cap)
    wanted = lax.all_to_all(request, "space", split_axis=1, concat_axis=1, tiled=True)
    returned = lax.all_to_all(
        jax.vmap(lambda image, index: image[index])(images, wanted),
        "space",
        split_axis=1,
        concat_axis=1,
        tiled=True,
    )
    returned = returned.reshape(subj_dev, spaces * cap, plane, depth_z)
    read_slot = jnp.minimum(slot, spaces * cap - 1)
    fetched = jax.vmap(lambda table, index: table[index])(returned, read_slot)
    live = alive.astype(jnp.float32)
    brick = fetched.astype(jnp.float32).reshape(subj_dev, rows_dev, BX, BY, depth_z)
    frac = weights.astype(jnp.float32).reshape(3, subj_dev, rows_dev, BX, BY, depth_z)
    warped = trilinear(brick, frac[0], frac[1], frac[2]) * live[:, :, None, None, None]
    grads = gradients(warped)
    whole = lax.all_gather(template, "subj", axis=1, tiled=True)
    current = whole.reshape(rows_dev, BX, BY, depth_z)
    field = velocity.reshape(3, subj_dev, rows_dev, BX, BY, depth_z)
    piece = plane // groups
    result = template
    for step in range(ITERS):
        predicted = predict(warped, grads, field)
        ratio = (predicted - current[None]) / (
            grads[0] * grads[0] + grads[1] * grads[1] + grads[2] * grads[2] + ridge
        )
        update = grads * ratio[None]
        padded = extended(update, (("space", 2),), 1)
        rowwise = 0.25 * padded[:, :, :-2] + 0.5 * update + 0.25 * padded[:, :, 2:]
        field = field - smooth_z(rowwise)
        local_sum = jnp.sum(predict(warped, grads, field), axis=0).reshape(rows_dev, plane, depth_z)
        total = lax.psum(local_sum, "subj") / subjects
        current = total.reshape(rows_dev, BX, BY, depth_z)
        result = lax.dynamic_slice_in_dim(total, lax.axis_index("subj") * piece, piece, 1)
    return (field.reshape(3, subj_dev, rows_dev, plane, depth_z), result)


def solution(mesh):
    in_specs = (
        P("subj", "space", None, None),
        P(None, "subj", "space", None, None),
        P(None, "subj", "space", None, None),
        P("space", "subj", None),
        P("subj", "space", None),
        P("subj", "space"),
        P("subj", "space"),
    )
    out_specs = (P(None, "subj", "space", None, None), P("space", "subj", None))
    return jax.shard_map(body, mesh=mesh, in_specs=in_specs, out_specs=out_specs, check_vma=False)
```

profile of v0, /device:TPU:8, one launch (start us, length us, event | category | flops | bytes accessed | tf_op | source)
XLA Modules:
  0.0 271.8 jit_solution(7685412767636631632)
XLA Ops:
  7.2 0.7 subtract_bitcast_fusion
  8.0 0.8 fusion.32
  8.9 0.9 fusion.31
  9.7 0.8 fusion.38
  10.6 0.8 reshape.242
  11.4 6.4 %scatter_fusion = s32[2,128]{1,0:T(2,128)S(1)} fusion(s32[2,128]{1,0:T(2,128)S(1)} %broadcast_in_dim.10, s32[128]{0:T(128)S(1)} %reshape.240, s32[128]{0:T(128)S(1)} %reshape.242), kind=kCustom, calls=%fused_computation.2 | custom fusion | bytes 2560 | tf_op jit(solution)/shard_map/scatter | solution.py:93
  17.9 20.2 %all_to_all.10 = s32[2,32,4]{2,0,1:T(2,128)S(1)} all-to-all(s32[2,32,4]{2,0,1:T(2,128)S(1)} %copy.24), channel_id=1, replica_groups=mesh['subj'=8,'space'=32] {'space'}, dimensions={1} | all-to-all | bytes 2048 | tf_op jit(solution)/shard_map/all_to_all | solution.py:95
  38.4 1.2 gather_fusion
  39.7 1.1 copy.29
  40.8 5.8 %all-to-all-start.1 = ((bf16[2,32,4,16,128]{4,3,2,0,1:T(8,128)(2,1)}), bf16[2,32,4,16,128]{4,3,2,0,1:T(8,128)(2,1)}, u32[]{:S(2)}, u32[]{:S(2)}) async-start(bf16[2,32,4,16,128]{4,3,2,0,1:T(8,128)(2,1)} %copy.29), calls=%async_computation.1 | async-start | bytes 2097152 | tf_op jit(solution)/shard_map/all_to_all | solution.py:96
  46.8 13.5 %all_gather.3 = f32[64,16,128]{2,0,1:T(8,128)S(1)} all-gather(f32[64,2,128]{2,0,1:T(8,128)S(1)} %copy.31), channel_id=1, replica_groups=mesh['subj'=8,'space'=32] {'subj'}, dimensions={1}, use_global_device_ids=true | all-gather | bytes 589824 | tf_op jit(solution)/shard_map/all_gather | solution.py:111
  60.2 1.2 copy.32
  61.4 1.6 fusion.52
  63.0 1.1 copy-done.8
  64.0 1.7 fusion.51
  65.8 5.9 %all-to-all-done.1 = bf16[2,32,4,16,128]{4,3,2,0,1:T(8,128)(2,1)} async-done(((bf16[2,32,4,16,128]{4,3,2,0,1:T(8,128)(2,1)}), bf16[2,32,4,16,128]{4,3,2,0,1:T(8,128)(2,1)}, u32[]{:S(2)}, u32[]{:S(2)}) %all-to-all-start.1) | async-done | bytes 1048608 | tf_op jit(solution)/shard_map/all_to_all | solution.py:96
  71.7 1.4 copy.30
  73.1 0.9 gather_fusion.1
  74.4 0.3 slice.170
  75.0 1.0 pad_slice_fusion.1
  76.0 0.6 pad_slice_fusion.3
  76.7 2.3 fusion.12
  79.0 0.6 fusion.53
  79.7 0.4 fusion.54
  80.4 0.5 copy-done.14
  81.2 0.6 copy-done.16
  81.9 1.9 subtract_divide_fusion.1
  83.9 0.9 broadcast_multiply_fusion.1
  84.9 5.0 %collective-permute-start = (f32[3,2,1,4,4,128]{5,4,3,2,1,0:T(4,128)S(1)}, f32[3,2,1,4,4,128]{5,4,3,2,1,0:T(4,128)S(1)}, u32[]{:S(2)}, u32[]{:S(2)}) collective-permute-start(f32[3,2,1,4,4,128]{5,4,3,2,1,0:T(4,128)S(1)} %get-tuple-element.17), channel_id=1, source_target_pairs={{0,1},{1,2},{2,3},{3,4},{4,5},{5,6},{6,7},{7,8},{8,9},{9,10},{10,1... | collective-permute-start | bytes 147464 | tf_op jit(solution)/shard_map/ppermute | solution.py:19
  89.9 3.1 %collective-permute-start.1 = (f32[3,2,1,4,4,128]{5,4,3,2,1,0:T(4,128)S(1)}, f32[3,2,1,4,4,128]{5,4,3,2,1,0:T(4,128)S(1)}, u32[]{:S(2)}, u32[]{:S(2)}) collective-permute-start(f32[3,2,1,4,4,128]{5,4,3,2,1,0:T(4,128)S(1)} %get-tuple-element.18), channel_id=1, source_target_pairs={{1,0},{2,1},{3,2},{4,3},{5,4},{6,5},{7,6},{8,7},{9,8},{10,9},{11,1... | collective-permute-start | bytes 147464 | tf_op jit(solution)/shard_map/ppermute | solution.py:22
  93.0 2.9 %collective-permute-done.1 = f32[3,2,1,4,4,128]{5,4,3,2,1,0:T(4,128)S(1)} collective-permute-done((f32[3,2,1,4,4,128]{5,4,3,2,1,0:T(4,128)S(1)}, f32[3,2,1,4,4,128]{5,4,3,2,1,0:T(4,128)S(1)}, u32[]{:S(2)}, u32[]{:S(2)}) %collective-permute-start.1) | collective-permute-done | bytes 49184 | tf_op jit(solution)/shard_map/ppermute | solution.py:22
  95.9 2.2 fusion.5
  98.2 2.1 fusion.49
  100.3 4.2 %add_subtract_fusion.1 = f32[3,2,64,4,4,128]{5,4,3,2,1,0:T(4,128)S(1)} fusion(f32[3,2,64,4,4,128]{5,4,3,2,1,0:T(4,128)S(1)} %bitcast.99, f32[3,2,64,4,4,127]{5,4,3,2,1,0:T(4,128)S(1)} %get-tuple-element.16, f32[3,2,64,4,4,127]{5,4,3,2,1,0:T(4,128)S(1)} %get-tuple-element.15, f32[3,2,1,4,4,128]{5,4,3,2,1,0:T(4,128)S(1)} %collective-permute-done.1, ...), kind=kLoop, calls=%fused_computation.17 | loop fusion | flops 10223616 | bytes 15777792 | tf_op jit(solution)/shard_map/sub | solution.py:124
  104.5 3.3 %fusion.45 = (f32[64,4,4,128]{3,2,1,0:T(4,128)}, f32[2,64,4,4,128]{4,3,2,1,0:T(4,128)}) fusion(f32[2,64,4,4,128]{4,3,2,1,0:T(4,128)S(1)} %get-tuple-element.6, f32[3,2,64,4,4,128]{5,4,3,2,1,0:T(4,128)S(1)} %add_subtract_fusion.1, f32[2,64,4,4,128]{4,3,2,1,0:T(4,128)S(1)} %fusion.12, f32[2,64,4,4,128]{4,3,2,1,0:T(4,128)S(1)} %get-tuple-element.5, ...), kind=kLoop, calls=%fused_computation.94 | loop fusion | flops 2228224 | bytes 9437184 | tf_op jit(solution)/shard_map/reduce_sum | solution.py:125
  107.9 65.1 %all-reduce.20.cloned.1.call-done = f32[64,16,128]{2,1,0:T(8,128)} async-done(((f32[64,16,128]{2,1,0:T(8,128)}), f32[64,16,128]{2,1,0:T(8,128)}) %all-reduce.20.cloned.1.call-update) | async-done | bytes 524304 | tf_op jit(solution)/shard_map/psum | solution.py:126
  173.0 1.1 broadcast_multiply_fusion.2
  174.1 2.6 subtract_divide_fusion
  176.8 0.9 broadcast_multiply_fusion
  177.6 3.5 %collective-permute-start.2 = (f32[3,2,1,4,4,128]{5,4,3,2,1,0:T(4,128)S(1)}, f32[3,2,1,4,4,128]{5,4,3,2,1,0:T(4,128)S(1)}, u32[]{:S(2)}, u32[]{:S(2)}) collective-permute-start(f32[3,2,1,4,4,128]{5,4,3,2,1,0:T(4,128)S(1)} %get-tuple-element.13), channel_id=1, source_target_pairs={{0,1},{1,2},{2,3},{3,4},{4,5},{5,6},{6,7},{7,8},{8,9},{9,10},{10,1... | collective-permute-start | bytes 147464 | tf_op jit(solution)/shard_map/ppermute | solution.py:19
  181.1 4.7 %collective-permute-start.3 = (f32[3,2,1,4,4,128]{5,4,3,2,1,0:T(4,128)S(1)}, f32[3,2,1,4,4,128]{5,4,3,2,1,0:T(4,128)S(1)}, u32[]{:S(2)}, u32[]{:S(2)}) collective-permute-start(f32[3,2,1,4,4,128]{5,4,3,2,1,0:T(4,128)S(1)} %get-tuple-element.14), channel_id=1, source_target_pairs={{1,0},{2,1},{3,2},{4,3},{5,4},{6,5},{7,6},{8,7},{9,8},{10,9},{11,1... | collective-permute-start | bytes 147464 | tf_op jit(solution)/shard_map/ppermute | solution.py:22
  185.8 1.5 collective-permute-done.3
  187.3 2.2 fusion.1
  189.6 2.1 fusion.47
  191.8 4.2 %add_subtract_fusion = f32[3,2,64,4,4,128]{5,4,3,2,1,0:T(4,128)S(1)} fusion(f32[3,2,64,4,4,128]{5,4,3,2,1,0:T(4,128)S(1)} %copy-done.5, f32[3,2,64,4,4,127]{5,4,3,2,1,0:T(4,128)S(1)} %get-tuple-element.12, f32[3,2,64,4,4,127]{5,4,3,2,1,0:T(4,128)S(1)} %get-tuple-element.11, f32[3,2,1,4,4,128]{5,4,3,2,1,0:T(4,128)S(1)} %collective-permute-done.3, ...), kind=kLoop, calls=%fused_computation.16 | loop fusion | flops 10223616 | bytes 15777792 | tf_op jit(solution)/shard_map/sub | solution.py:124
  196.0 2.3 fusion.15
  198.3 65.1 %all-reduce.22.cloned.1.call-done = f32[64,16,128]{2,1,0:T(8,128)} async-done(((f32[64,16,128]{2,1,0:T(8,128)}), f32[64,16,128]{2,1,0:T(8,128)}) %all-reduce.22.cloned.1.call-update) | async-done | bytes 524304 | tf_op jit(solution)/shard_map/psum | solution.py:126
  263.4 1.6 dynamic-slice_multiply_fusion
  (64 shorter events, 2.5 us)
Async XLA Ops:
  7.2 31.3 %copy-start = (bf16[2,64,16,128]{3,2,1,0:T(8,128)(2,1)S(1)}, bf16[2,64,16,128]{3,2,1,0:T(8,128)(2,1)}, u32[]{:S(2)}) copy-start(bf16[2,64,16,128]{3,2,1,0:T(8,128)(2,1)} %param.7) | copy-start | bytes 1572868
  38.4 8.3 %copy-start.20 = (f32[64,2,128]{2,1,0:T(2,128)S(1)}, f32[64,2,128]{2,1,0:T(2,128)}, u32[]{:S(2)}) copy-start(f32[64,2,128]{2,1,0:T(2,128)} %param.10) | copy-start | bytes 196612
  39.7 21.7 %copy-start.13 = (bf16[3,2,64,16,128]{4,3,2,1,0:T(8,128)(2,1)S(1)}, bf16[3,2,64,16,128]{4,3,2,1,0:T(8,128)(2,1)}, u32[]{:S(2)}) copy-start(bf16[3,2,64,16,128]{4,3,2,1,0:T(8,128)(2,1)} %param.9) | copy-start | bytes 4718596
  40.8 30.8 %all-to-all-start.1 = ((bf16[2,32,4,16,128]{4,3,2,0,1:T(8,128)(2,1)}), bf16[2,32,4,16,128]{4,3,2,0,1:T(8,128)(2,1)}, u32[]{:S(2)}, u32[]{:S(2)}) async-start(bf16[2,32,4,16,128]{4,3,2,0,1:T(8,128)(2,1)} %copy.29), calls=%async_computation.1 | async-start | bytes 2097152 | tf_op jit(solution)/shard_map/all_to_all | solution.py:96
  46.6 126.4 %all-reduce.20.cloned.1.call-start = ((), (), s32[]{:S(2)}) async-start(), calls=%async_computation.2 | async-start | bytes 1048576 | tf_op jit(solution)/shard_map/psum | solution.py:126
  61.4 2.6 copy-start.8
  75.0 1.6 copy-start.17
  75.0 1.6 copy-start.18
  79.6 1.2 copy-start.14
  79.6 1.5 copy-start.15
  79.7 2.1 copy-start.16
  79.7 2.2 copy-start.19
  80.4 24.1 %copy-start.6 = (f32[2,64,3,4,128]{4,3,2,1,0:T(4,128)}, f32[2,64,3,4,128]{4,3,2,1,0:T(4,128)S(1)}, u32[]{:S(2)}) copy-start(f32[2,64,3,4,128]{4,3,2,1,0:T(4,128)S(1)} %get-tuple-element.31) | copy-start | bytes 2359300
  83.9 1.0 copy-start.11
  83.9 20.6 %copy-start.2 = (f32[2,64,4,4,128]{4,3,2,1,0:T(4,128)}, f32[2,64,4,4,128]{4,3,2,1,0:T(4,128)S(1)}, u32[]{:S(2)}) copy-start(f32[2,64,4,4,128]{4,3,2,1,0:T(4,128)S(1)} %get-tuple-element.6) | copy-start | bytes 3145732
  84.9 8.1 %collective-permute-start = (f32[3,2,1,4,4,128]{5,4,3,2,1,0:T(4,128)S(1)}, f32[3,2,1,4,4,128]{5,4,3,2,1,0:T(4,128)S(1)}, u32[]{:S(2)}, u32[]{:S(2)}) collective-permute-start(f32[3,2,1,4,4,128]{5,4,3,2,1,0:T(4,128)S(1)} %get-tuple-element.17), channel_id=1, source_target_pairs={{0,1},{1,2},{2,3},{3,4},{4,5},{5,6},{6,7},{7,8},{8,9},{9,10},{10,1... | collective-permute-start | bytes 147464 | tf_op jit(solution)/shard_map/ppermute | solution.py:19
  89.9 6.0 %collective-permute-start.1 = (f32[3,2,1,4,4,128]{5,4,3,2,1,0:T(4,128)S(1)}, f32[3,2,1,4,4,128]{5,4,3,2,1,0:T(4,128)S(1)}, u32[]{:S(2)}, u32[]{:S(2)}) collective-permute-start(f32[3,2,1,4,4,128]{5,4,3,2,1,0:T(4,128)S(1)} %get-tuple-element.18), channel_id=1, source_target_pairs={{1,0},{2,1},{3,2},{4,3},{5,4},{6,5},{7,6},{8,7},{9,8},{10,9},{11,1... | collective-permute-start | bytes 147464 | tf_op jit(solution)/shard_map/ppermute | solution.py:22
  98.2 2.2 copy-start.9
  104.5 3.3 %copy-start.4 = (f32[3,2,64,4,4,128]{5,4,3,2,1,0:T(4,128)}, f32[3,2,64,4,4,128]{5,4,3,2,1,0:T(4,128)S(1)}, u32[]{:S(2)}) copy-start(f32[3,2,64,4,4,128]{5,4,3,2,1,0:T(4,128)S(1)} %add_subtract_fusion.1) | copy-start | bytes 9437188
  107.9 155.5 %all-reduce.22.cloned.1.call-start = ((), (), s32[]{:S(2)}) async-start(), calls=%async_computation.3 | async-start | bytes 1048576 | tf_op jit(solution)/shard_map/psum | solution.py:126
  174.1 2.7 copy-start.3
  174.1 2.7 copy-start.12
  177.6 8.2 %collective-permute-start.2 = (f32[3,2,1,4,4,128]{5,4,3,2,1,0:T(4,128)S(1)}, f32[3,2,1,4,4,128]{5,4,3,2,1,0:T(4,128)S(1)}, u32[]{:S(2)}, u32[]{:S(2)}) collective-permute-start(f32[3,2,1,4,4,128]{5,4,3,2,1,0:T(4,128)S(1)} %get-tuple-element.13), channel_id=1, source_target_pairs={{0,1},{1,2},{2,3},{3,4},{4,5},{5,6},{6,7},{7,8},{8,9},{9,10},{10,1... | collective-permute-start | bytes 147464 | tf_op jit(solution)/shard_map/ppermute | solution.py:19
  181.1 6.2 %collective-permute-start.3 = (f32[3,2,1,4,4,128]{5,4,3,2,1,0:T(4,128)S(1)}, f32[3,2,1,4,4,128]{5,4,3,2,1,0:T(4,128)S(1)}, u32[]{:S(2)}, u32[]{:S(2)}) collective-permute-start(f32[3,2,1,4,4,128]{5,4,3,2,1,0:T(4,128)S(1)} %get-tuple-element.14), channel_id=1, source_target_pairs={{1,0},{2,1},{3,2},{4,3},{5,4},{6,5},{7,6},{8,7},{9,8},{10,9},{11,1... | collective-permute-start | bytes 147464 | tf_op jit(solution)/shard_map/ppermute | solution.py:22
  189.6 2.2 copy-start.5
  191.8 4.2 %copy-start.7 = (f32[2,64,3,4,128]{4,3,2,1,0:T(4,128)S(1)}, f32[2,64,3,4,128]{4,3,2,1,0:T(4,128)}, u32[]{:S(2)}) copy-start(f32[2,64,3,4,128]{4,3,2,1,0:T(4,128)} %copy-done.6) | copy-start | bytes 2359300
  191.8 73.2 %copy-start.1 = (bf16[2,64,16,128]{3,2,1,0:T(8,128)(2,1)S(1)}, bf16[2,64,16,128]{3,2,1,0:T(8,128)(2,1)}, u32[]{:S(2)}) copy-start(bf16[2,64,16,128]{3,2,1,0:T(8,128)(2,1)} %param.7) | copy-start | bytes 1572868
  196.0 2.3 copy-start.10
Sparse Core Ops, SparseCore 0:
  108.0 64.9 all-reduce.19
  198.4 64.9 all-reduce.21
where the time goes:
time: 272 us
  waiting for transfers between devices  140 us (51%)
  blocking collectives  33.6 us (12%)
  other arithmetic  33.1 us (12%)
  local copies, waits for them, and re-layouts  28 us (10%)
  starting transfers between devices  22.2 us (8%)
  between operations  14.5 us (5%)
    psum x2, waiting for transfers between devices, body(): total = lax.psum(local_sum, 'subj') / subjects  130 us
    all_to_all x1, blocking collectives, body(): lax.all_to_all(request, 'space', split_axis=1, concat_axis=1, tiled=True)  20.2 us
    all_gather x1, blocking collectives, body(): whole = lax.all_gather(template, 'subj', axis=1, tiled=True)  13.5 us
    ppermute x2, starting transfers between devices, extended(): lax.ppermute(lax.slice_in_dim(block, block.shape[dim] - width, None, axis...  8.51 us
    sub x2, other arithmetic, body(): field = field - smooth_z(rowwise)  8.33 us
    ppermute x2, starting transfers between devices, extended(): lax.ppermute(lax.slice_in_dim(block, 0, width, axis=dim), axis, backward)  7.79 us
    scatter x1, local copies, waits for them, and re-layouts, body(): request.at[jnp.arange(subj_dev)[:, None], slot].set(local_rows, mode='drop')  6.43 us
    all_to_all x1, waiting for transfers between devices, body(): lax.all_to_all(jax.vmap(lambda image, index: image[index])(images, wanted...  5.9 us
  transfers between devices with their start and end apart: 7, of which 5 were waited for; matrix products, arithmetic and copies ran while one was open for 2% of the time, Pallas kernels for 0%

commit v1 on v0

v1 whole, which is shorter than its diff:
```python
import functools

import jax
import jax.numpy as jnp
from jax import lax
from jax.experimental import pallas as pl
from jax.experimental.pallas import tpu as pltpu
from jax.sharding import PartitionSpec as P

MESH = pl.DeviceIdType.MESH
F32 = jnp.float32
I32 = jnp.int32
PLANE = 16
LANES = 128


def kernel(
    nj, ny, nz, rows, cap,
    img_h, vel_h, wts_h, tin_ref, own_ref, loc_ref, cnt_ref,
    out_h, tout_ref,
    img, wts, f, sendb, recvb0, recvb1, warp, g, q, r, pr, cur0, cur1, total,
    tsend, trecv, req, rreq, slot_v, rreq_s, slot_s, edge, halo,
    part, crecv, xsend, xrecv, fsend, frecv, fx, fxrecv,
    in_sem, out_sem, tsend_sem, trecv_sem, qsend_sem, qrecv_sem, loc_sem,
    bsend_sem, brecv_sem, hsend_sem, hrecv_sem,
    csend_sem, crecv_sem, xsend_sem, xrecv_sem, gsend_sem, grecv_sem,
    asend_sem, arecv_sem, fsend_sem, frecv_sem, ysend_sem, yrecv_sem,
):
    ns = ny * nz
    nx = nj // 2
    pd = PLANE // nj
    sj = lax.axis_index("subj")
    sp = lax.axis_index("space")
    x, c = sj // 2, sj % 2
    y, z = sp // nz, sp % nz
    mate = x * 2 + (1 - c)
    recvb = (recvb0, recvb1)
    half = rows // 2
    piece = rows // nj

    def peer(j):
        dy, zi = j % ny, j // ny
        dz = jnp.where(zi % 2 == 1, (zi + 1) // 2, nz - zi // 2)
        return ((y + dy) % ny) * nz + (z + dz) % nz

    img_in = pltpu.make_async_copy(img_h, img, in_sem.at[0])
    img_in.start()
    wts_in = pltpu.make_async_copy(wts_h, wts, in_sem.at[1])
    wts_in.start()
    vel_in = pltpu.make_async_copy(vel_h, f, in_sem.at[2])
    vel_in.start()

    barrier = pltpu.get_barrier_semaphore()

    def greet(j, carry):
        pl.semaphore_signal(barrier, inc=1, device_id=(sj, peer(j)), device_id_type=MESH)
        return carry

    def greet_subj(i, carry):
        pl.semaphore_signal(barrier, inc=1, device_id=((sj + i) % nj, sp), device_id_type=MESH)
        return carry

    lax.fori_loop(1, ns, greet, 0)
    lax.fori_loop(1, nj, greet_subj, 0)

    for p in range(pd):
        tsend[p] = tin_ref[pl.ds(p, rows, stride=pd), :]

    i0 = lax.broadcasted_iota(I32, (rows, rows), 0)
    i1 = lax.broadcasted_iota(I32, (rows, rows), 1)
    who = lax.broadcasted_iota(I32, (ns, rows), 0)
    lane = lax.broadcasted_iota(I32, (ns, LANES), 1)
    asked = jnp.zeros((ns, LANES), I32)
    slot_v[...] = jnp.zeros_like(slot_v)
    for s in range(2):
        count = cnt_ref[0, s]
        first = count // 2
        last = rows - (count - first)
        row = own_ref[s]
        col = jnp.sum(jnp.where(i0 == i1, row, 0), axis=1, keepdims=True)
        alive0 = (i0 < first) | (i0 >= last)
        hit = (col == row) & (i0 < i1) & alive0
        before = jnp.sum(jnp.where(hit, 1, 0), axis=0, keepdims=True)
        t1 = i1[0:1, :]
        alive1 = (t1 < first) | (t1 >= last)
        slot = jnp.where(alive1, row * cap + before, 0)
        slot_v[s, :, 0:rows] = slot
        place = jnp.where(alive1, before, cap)
        for k in range(cap):
            mine = (row == who) & (place == k)
            column = jnp.sum(jnp.where(mine, loc_ref[s : s + 1, :], 0), axis=1, keepdims=True)
            asked = asked + jnp.where(lane == s * cap + k, column, 0)
    for d in range(ns):
        req[d] = asked[d : d + 1, :]
    slots_in = pltpu.make_async_copy(slot_v, slot_s, loc_sem.at[0])
    slots_in.start()

    pl.semaphore_wait(barrier, ns - 1 + nj - 1)

    def ask(j):
        d = peer(j)
        return pltpu.make_async_remote_copy(
            src_ref=req.at[d], dst_ref=rreq.at[sp],
            send_sem=qsend_sem.at[j], recv_sem=qrecv_sem.at[sp],
            device_id=(sj, d), device_id_type=MESH,
        )

    def asked_by(d):
        return pltpu.make_async_remote_copy(
            src_ref=req.at[d], dst_ref=rreq.at[d],
            send_sem=qsend_sem.at[0], recv_sem=qrecv_sem.at[d],
            device_id=(sj, sp), device_id_type=MESH,
        )

    def start_ask(j, carry):
        ask(j).start()
        return carry

    lax.fori_loop(1, ns, start_ask, 0)
    own_ask = pltpu.make_async_copy(req.at[sp], rreq.at[sp], loc_sem.at[1])
    own_ask.start()

    def plane_copy(i):
        return pltpu.make_async_remote_copy(
            src_ref=tsend, dst_ref=trecv.at[sj],
            send_sem=tsend_sem.at[i], recv_sem=trecv_sem.at[sj],
            device_id=((sj + i) % nj, sp), device_id_type=MESH,
        )

    def start_planes(i, carry):
        plane_copy(i).start()
        return carry

    lax.fori_loop(1, nj, start_planes, 0)

    def wait_ask(j, carry):
        asked_by(peer(j)).wait_recv()
        return carry

    own_ask.wait()
    lax.fori_loop(1, ns, wait_ask, 0)
    rreq_in = pltpu.make_async_copy(rreq, rreq_s, loc_sem.at[2])
    rreq_in.start()
    img_in.wait()
    rreq_in.wait()

    def brick(s, j):
        d = peer(j)
        return pltpu.make_async_remote_copy(
            src_ref=sendb.at[s, pl.ds(d * cap, cap)], dst_ref=recvb[s].at[pl.ds(sp * cap, cap)],
            send_sem=bsend_sem.at[s, j], recv_sem=brecv_sem.at[s, sp],
            device_id=(sj, d), device_id_type=MESH,
        )

    def brick_from(s, d):
        return pltpu.make_async_remote_copy(
            src_ref=sendb.at[s, pl.ds(d * cap, cap)], dst_ref=recvb[s].at[pl.ds(d * cap, cap)],
            send_sem=bsend_sem.at[s, 0], recv_sem=brecv_sem.at[s, d],
            device_id=(sj, sp), device_id_type=MESH,
        )

    for s in range(2):

        def gather(j, carry):
            d = peer(j)
            for k in range(cap):
                sendb[s, d * cap + k] = img[s, rreq_s[d, 0, s * cap + k]]

            @pl.when(j >= 2)
            def _():
                brick(s, j - 1).start()

            return carry

        lax.fori_loop(1, ns, gather, 0)
        for k in range(cap):
            recvb[s][sp * cap + k] = img[s, rreq_s[sp, 0, s * cap + k]]
        brick(s, ns - 1).start()

    def wait_planes(i, carry):
        other = (sj + i) % nj
        pltpu.make_async_remote_copy(
            src_ref=tsend, dst_ref=trecv.at[other],
            send_sem=tsend_sem.at[0], recv_sem=trecv_sem.at[other],
            device_id=(sj, sp), device_id_type=MESH,
        ).wait_recv()
        return carry

    lax.fori_loop(1, nj, wait_planes, 0)
    trecv[sj] = tsend[...]
    for j in range(nj):
        for p in range(pd):
            cur0[pl.ds(j * pd + p, rows, stride=PLANE), :] = trecv[j, p]

    @pl.when(sp == 0)
    def _():
        halo[:, 0] = jnp.zeros_like(halo[:, 0])

    @pl.when(sp == ns - 1)
    def _():
        halo[:, 1] = jnp.zeros_like(halo[:, 1])

    wts_in.wait()
    vel_in.wait()
    slots_in.wait()

    lanes = lax.broadcasted_iota(I32, (8, LANES), 1)
    subs = lax.broadcasted_iota(I32, (8, LANES), 0)
    low = subs < 4
    y_top = subs % 4 == 3
    y_bot = subs % 4 == 0
    z_top = lanes == LANES - 1
    z_bot = lanes == 0

    def up_z(v):
        return jnp.where(z_top, 0.0, pltpu.roll(v, LANES - 1, 1))

    def down_z(v):
        return jnp.where(z_bot, 0.0, pltpu.roll(v, 1, 1))

    def up_y(v):
        return jnp.where(y_top, 0.0, pltpu.roll(v, 7, 0))

    def down_y(v):
        return jnp.where(y_bot, 0.0, pltpu.roll(v, 1, 0))

    def up_x(pair):
        a, b = [pltpu.roll(v, 4, 0) for v in pair]
        return [jnp.where(low, a, b), jnp.where(low, b, 0.0)]

    def pair_of(value):
        return [value[0:8], value[8:16]]

    def put(ref, index, pair):
        ref[index + (slice(0, 8),)] = pair[0]
        ref[index + (slice(8, 16),)] = pair[1]

    both = (0, 1)

    for s in range(2):

        def arrived(j, carry):
            brick_from(s, peer(j)).wait_recv()
            return carry

        lax.fori_loop(1, ns, arrived, 0)
        count = cnt_ref[0, s]
        first = count // 2
        last = rows - (count - first)

        def warp_tile(t, carry):
            b00 = pair_of(recvb[s][slot_s[s, 0, t]].astype(F32))
            wx, wy, wz = [pair_of(wts[a, s, t].astype(F32)) for a in range(3)]
            live = jnp.where((t < first) | (t >= last), 1.0, 0.0).astype(F32)
            d00 = [up_z(v) - v for v in b00]
            b01, d01 = [up_y(v) for v in b00], [up_y(v) for v in d00]
            b10, d10 = up_x(b00), up_x(d00)
            b11, d11 = up_x(b01), up_x(d01)
            w = []
            for i in both:
                l00 = b00[i] + wz[i] * d00[i]
                l01 = b01[i] + wz[i] * d01[i]
                l10 = b10[i] + wz[i] * d10[i]
                l11 = b11[i] + wz[i] * d11[i]
                m0 = l00 + wy[i] * (l01 - l00)
                m1 = l10 + wy[i] * (l11 - l10)
                w.append((m0 + wx[i] * (m1 - m0)) * live)
            h = [0.5 * v for v in w]
            ra, rb = [pltpu.roll(v, 4, 0) for v in h]
            mid = jnp.where(low, ra, rb)
            gx = [mid - jnp.where(low, 0.0, ra), jnp.where(low, rb, 0.0) - mid]
            gy = [up_y(v) - down_y(v) for v in h]
            gz = [up_z(v) - down_z(v) for v in h]
            here = pl.multiple_of(t * PLANE, PLANE)
            now = pair_of(cur0[pl.ds(here, PLANE), :])
            fx0, fy0, fz0 = [pair_of(f[a, s, t]) for a in range(3)]
            qq, rr = [], []
            for i in both:
                sq = gx[i] * gx[i] + gy[i] * gy[i] + gz[i] * gz[i]
                inverse = 1.0 / (16.0 * sq + 4.0)
                pred = w[i] + (gx[i] * fx0[i] + gy[i] * fy0[i]) + gz[i] * fz0[i]
                qq.append(inverse)
                rr.append((pred - now[i]) * inverse)
            put(warp, (s, t), w)
            put(g, (0, s, t), gx)
            put(g, (1, s, t), gy)
            put(g, (2, s, t), gz)
            put(q, (s, t), qq)
            put(r, (s, t), rr)
            return carry

        lax.fori_loop(0, rows, warp_tile, 0)

    def first_ratio(s, t):
        return pair_of(r[s, t])

    def second_ratio(s, t):
        here = pl.multiple_of(t * PLANE, PLANE)
        now = pair_of(cur1[pl.ds(here, PLANE), :])
        p1 = pair_of(pr[s, t])
        qq = pair_of(q[s, t])
        return [(p1[i] - now[i]) * qq[i] for i in both]

    def edge_copy(it, side):
        d = sp - 1 if side == 0 else sp + 1
        return pltpu.make_async_remote_copy(
            src_ref=edge.at[it, side], dst_ref=halo.at[it, 1 - side],
            send_sem=hsend_sem.at[it, side], recv_sem=hrecv_sem.at[it, 1 - side],
            device_id=(sj, d), device_id_type=MESH,
        )

    def halo_in(it, side):
        return pltpu.make_async_remote_copy(
            src_ref=edge.at[it, side], dst_ref=halo.at[it, side],
            send_sem=hsend_sem.at[it, side], recv_sem=hrecv_sem.at[it, side],
            device_id=(sj, sp), device_id_type=MESH,
        )

    def iterate(it):
        ratio = first_ratio if it == 0 else second_ratio

        def update(s, t):
            rr = ratio(s, t)
            out = []
            for a in range(3):
                gg = pair_of(g[a, s, t])
                out += [gg[0] * rr[0], gg[1] * rr[1]]
            return out

        for s in range(2):
            for side, t in ((0, 0), (1, rows - 1)):
                u = update(s, t)
                for a in range(3):
                    put(edge, (it, side, a, s), u[2 * a : 2 * a + 2])

        @pl.when(sp > 0)
        def _():
            edge_copy(it, 0).start()

        @pl.when(sp < ns - 1)
        def _():
            edge_copy(it, 1).start()

        def advance(s, t, v):
            new = []
            for a in range(3):
                old = pair_of(f[a, s, t])
                out = []
                for i in both:
                    value = v[2 * a + i]
                    two = value + down_z(value)
                    out.append(old[i] - (two + jnp.where(z_top, value, pltpu.roll(two, LANES - 1, 1))))
                put(f, (a, s, t), out)
                new.append(out)
            w = pair_of(warp[s, t])
            gg = [pair_of(g[a, s, t]) for a in range(3)]
            pred = [
                w[i] + (gg[0][i] * new[0][i] + gg[1][i] * new[1][i]) + gg[2][i] * new[2][i]
                for i in both
            ]
            if it == 0:
                put(pr, (s, t), pred)
            here = pl.multiple_of(t * PLANE, PLANE)
            if s == 0:
                total[pl.ds(here, 8), :] = pred[0]
                total[pl.ds(here + 8, 8), :] = pred[1]
            else:
                total[pl.ds(here, 8), :] = total[pl.ds(here, 8), :] + pred[0]
                total[pl.ds(here + 8, 8), :] = total[pl.ds(here + 8, 8), :] + pred[1]

        for s in range(2):
            u0, u1 = update(s, 0), update(s, 1)
            before = [a + b for a, b in zip(u0, u1)]

            def inner(t, carry):
                before, u = list(carry[:6]), list(carry[6:])
                after = update(s, t + 1)
                two = [a + b for a, b in zip(u, after)]
                advance(s, t, [a + b for a, b in zip(before, two)])
                return tuple(two + after)

            lax.fori_loop(1, rows - 1, inner, tuple(before + u1))

        @pl.when(sp > 0)
        def _():
            halo_in(it, 0).wait_recv()

        @pl.when(sp < ns - 1)
        def _():
            halo_in(it, 1).wait_recv()

        for s in range(2):
            for side, t, near in ((0, 0, 1), (1, rows - 1, rows - 2)):
                u, v = update(s, t), update(s, near)
                far = []
                for a in range(3):
                    far += pair_of(halo[it, side, a, s])
                advance(s, t, [(far[n] + u[n]) + (u[n] + v[n]) for n in range(6)])

    iterate(0)

    mine = c * half * PLANE
    other = (1 - c) * half * PLANE
    span = half * PLANE
    block = piece * PLANE

    to_mate = pltpu.make_async_remote_copy(
        src_ref=total.at[pl.ds(other, span)], dst_ref=crecv,
        send_sem=csend_sem.at[0], recv_sem=crecv_sem.at[0],
        device_id=(mate, sp), device_id_type=MESH,
    )
    to_mate.start()
    to_mate.wait_recv()
    xsend[...] = total[pl.ds(mine, span), :] + crecv[...]

    def chip(i):
        return (x + i) % nx

    for i in range(1, nx):
        pltpu.make_async_remote_copy(
            src_ref=xsend.at[pl.ds(chip(i) * block, block)], dst_ref=xrecv.at[x],
            send_sem=xsend_sem.at[i], recv_sem=xrecv_sem.at[x],
            device_id=(chip(i) * 2 + c, sp), device_id_type=MESH,
        ).start()
    acc = xsend[pl.ds(x * block, block), :]
    for i in range(1, nx):
        pltpu.make_async_remote_copy(
            src_ref=xrecv.at[0], dst_ref=xrecv.at[chip(i)],
            send_sem=xsend_sem.at[i], recv_sem=xrecv_sem.at[chip(i)],
            device_id=(sj, sp), device_id_type=MESH,
        ).wait_recv()
        acc = acc + xrecv[chip(i)]
    scale = 1.0 / (2.0 * nj)
    home = mine + x * block
    part[...] = acc * scale

    def spread(i):
        return pltpu.make_async_remote_copy(
            src_ref=part, dst_ref=cur1.at[pl.ds(home, block)],
            send_sem=gsend_sem.at[i], recv_sem=grecv_sem.at[x],
            device_id=(chip(i) * 2 + c, sp), device_id_type=MESH,
        )

    def spread_mate(src, where, n):
        return pltpu.make_async_remote_copy(
            src_ref=src, dst_ref=cur1.at[pl.ds(where, block)],
            send_sem=asend_sem.at[n], recv_sem=arecv_sem.at[n],
            device_id=(mate, sp), device_id_type=MESH,
        )

    for i in range(1, nx):
        spread(i).start()
    spread_mate(part, home, 0).start()
    cur1[pl.ds(home, block), :] = acc * scale
    for i in range(1, nx):
        where = mine + chip(i) * block
        pltpu.make_async_remote_copy(
            src_ref=part, dst_ref=cur1.at[pl.ds(where, block)],
            send_sem=gsend_sem.at[i], recv_sem=grecv_sem.at[chip(i)],
            device_id=(sj, sp), device_id_type=MESH,
        ).wait_recv()
        spread_mate(cur1.at[pl.ds(where, block)], where, i).start()
    for i in range(nx):
        where = other + chip(i) * block
        spread_mate(part, where, i).wait_recv()

    to_mate.wait_send()

    iterate(1)

    vel_out = pltpu.make_async_copy(f, out_h, out_sem.at[0])
    vel_out.start()

    for cc in range(2):
        for xx in range(nx):
            for p in range(pd):
                plane = (2 * xx + cc) * pd + p
                fsend[cc, xx, p] = total[pl.ds(plane, rows, stride=PLANE), :]
    planes_to_mate = pltpu.make_async_remote_copy(
        src_ref=fsend.at[1 - c], dst_ref=frecv,
        send_sem=fsend_sem.at[0], recv_sem=frecv_sem.at[0],
        device_id=(mate, sp), device_id_type=MESH,
    )
    planes_to_mate.start()
    planes_to_mate.wait_recv()
    fx[...] = fsend[c] + frecv[...]
    for i in range(1, nx):
        pltpu.make_async_remote_copy(
            src_ref=fx.at[chip(i)], dst_ref=fxrecv.at[x],
            send_sem=ysend_sem.at[i], recv_sem=yrecv_sem.at[x],
            device_id=(chip(i) * 2 + c, sp), device_id_type=MESH,
        ).start()
    acc = fx[x]
    for i in range(1, nx):
        pltpu.make_async_remote_copy(
            src_ref=fxrecv.at[0], dst_ref=fxrecv.at[chip(i)],
            send_sem=ysend_sem.at[i], recv_sem=yrecv_sem.at[chip(i)],
            device_id=(sj, sp), device_id_type=MESH,
        ).wait_recv()
        acc = acc + fxrecv[chip(i)]
    for p in range(pd):
        tout_ref[pl.ds(p, rows, stride=pd), :] = acc[p] * scale

    def sent_ask(j, carry):
        ask(j).wait_send()
        brick(0, j).wait_send()
        brick(1, j).wait_send()
        return carry

    lax.fori_loop(1, ns, sent_ask, 0)

    def sent_planes(i, carry):
        plane_copy(i).wait_send()
        return carry

    lax.fori_loop(1, nj, sent_planes, 0)
    for it in range(2):

        @pl.when(sp > 0)
        def _():
            edge_copy(it, 0).wait_send()

        @pl.when(sp < ns - 1)
        def _():
            edge_copy(it, 1).wait_send()

    planes_to_mate.wait_send()
    for i in range(nx):
        spread_mate(part, home, i).wait_send()
    for i in range(1, nx):
        spread(i).wait_send()
        pltpu.make_async_remote_copy(
            src_ref=xsend.at[pl.ds(chip(i) * block, block)], dst_ref=xrecv.at[x],
            send_sem=xsend_sem.at[i], recv_sem=xrecv_sem.at[x],
            device_id=(chip(i) * 2 + c, sp), device_id_type=MESH,
        ).wait_send()
        pltpu.make_async_remote_copy(
            src_ref=fx.at[chip(i)], dst_ref=fxrecv.at[x],
            send_sem=ysend_sem.at[i], recv_sem=yrecv_sem.at[x],
            device_id=(chip(i) * 2 + c, sp), device_id_type=MESH,
        ).wait_send()
    vel_out.wait()


def body(nj, ny, nz, images, velocity, weights, template, owners, local_rows, tile_counts):
    ns = ny * nz
    nx = nj // 2
    rows = images.shape[1]
    pd = template.shape[1]
    cap = 2 * rows // ns
    slots = ns * cap
    brick = (PLANE, LANES)
    piece = rows // nj * PLANE
    vmem = pl.BlockSpec(memory_space=pltpu.VMEM)
    smem = pl.BlockSpec(memory_space=pltpu.SMEM)
    away = pl.BlockSpec(memory_space=pl.ANY)
    bf16 = jnp.bfloat16
    dma = pltpu.SemaphoreType.DMA
    field, planes = pl.pallas_call(
        functools.partial(kernel, nj, ny, nz, rows, cap),
        out_shape=(
            jax.ShapeDtypeStruct(velocity.shape, F32),
            jax.ShapeDtypeStruct((rows * pd, LANES), F32),
        ),
        in_specs=[away, away, away, vmem, vmem, vmem, smem],
        out_specs=(away, vmem),
        scratch_shapes=[
            pltpu.VMEM((2, rows) + brick, bf16),
            pltpu.VMEM((3, 2, rows) + brick, bf16),
            pltpu.VMEM((3, 2, rows) + brick, F32),
            pltpu.VMEM((2, slots) + brick, bf16),
            pltpu.VMEM((slots,) + brick, bf16),
            pltpu.VMEM((slots,) + brick, bf16),
            pltpu.VMEM((2, rows) + brick, F32),
            pltpu.VMEM((3, 2, rows) + brick, F32),
            pltpu.VMEM((2, rows) + brick, F32),
            pltpu.VMEM((2, rows) + brick, F32),
            pltpu.VMEM((2, rows) + brick, F32),
            pltpu.VMEM((rows * PLANE, LANES), F32),
            pltpu.VMEM((rows * PLANE, LANES), F32),
            pltpu.VMEM((rows * PLANE, LANES), F32),
            pltpu.VMEM((pd, rows, LANES), F32),
            pltpu.VMEM((nj, pd, rows, LANES), F32),
            pltpu.VMEM((ns, 1, LANES), I32),
            pltpu.VMEM((ns, 1, LANES), I32),
            pltpu.VMEM((2, 1, LANES), I32),
            pltpu.SMEM((ns, 1, LANES), I32),
            pltpu.SMEM((2, 1, LANES), I32),
            pltpu.VMEM((2, 2, 3, 2) + brick, F32),
            pltpu.VMEM((2, 2, 3, 2) + brick, F32),
            pltpu.VMEM((piece, LANES), F32),
            pltpu.VMEM((rows // 2 * PLANE, LANES), F32),
            pltpu.VMEM((rows // 2 * PLANE, LANES), F32),
            pltpu.VMEM((nx, piece, LANES), F32),
            pltpu.VMEM((2, nx, pd, rows, LANES), F32),
            pltpu.VMEM((nx, pd, rows, LANES), F32),
            pltpu.VMEM((nx, pd, rows, LANES), F32),
            pltpu.VMEM((nx, pd, rows, LANES), F32),
            dma((3,)), dma((1,)), dma((nj,)), dma((nj,)), dma((ns,)), dma((ns,)), dma((3,)),
            dma((2, ns)), dma((2, ns)), dma((2, 2)), dma((2, 2)),
            dma((1,)), dma((1,)), dma((nx,)), dma((nx,)), dma((nx,)), dma((nx,)),
            dma((nx,)), dma((nx,)), dma((1,)), dma((1,)), dma((nx,)), dma((nx,)),
        ],
        compiler_params=pltpu.CompilerParams(
            collective_id=0, has_side_effects=True, vmem_limit_bytes=56 * 1024 * 1024
        ),
        name="demons",
    )(
        images, velocity, weights, template.reshape(rows * pd, LANES),
        jnp.swapaxes(owners, 1, 2), local_rows, tile_counts.T,
    )
    return field, planes.reshape(template.shape)


def solution(mesh):
    nj, ns = mesh.shape["subj"], mesh.shape["space"]
    nz = 8 if ns % 8 == 0 else 2
    in_specs = (
        P("subj", "space", None, None),
        P(None, "subj", "space", None, None),
        P(None, "subj", "space", None, None),
        P("space", "subj", None),
        P("subj", "space", None),
        P("subj", "space"),
        P("subj", "space"),
    )
    out_specs = (P(None, "subj", "space", None, None), P("space", "subj", None))
    return jax.shard_map(
        functools.partial(body, nj, ns // nz, nz),
        mesh=mesh, in_specs=in_specs, out_specs=out_specs, check_vma=False,
    )
```

time: 272 us -> 127 us (0.47)
  waiting for transfers between devices: 140 us -> 0 us
  Pallas kernels: 0 us -> 120 us
  blocking collectives: 33.6 us -> 0 us
  other arithmetic: 33.1 us -> 0 us
  local copies, waits for them, and re-layouts: 28 us -> 4.61 us
  starting transfers between devices: 22.2 us -> 0 us
  between operations: 14.5 us -> 0.65 us
    psum x2 -> x0, waiting for transfers between devices: 130 us -> none  [body(): total = lax.psum(local_sum, 'subj') / subjects]
    pallas_call x0 -> x1, Pallas kernels: none -> 120 us  [body(): pl.pallas_call(functools.partial(kernel, nj, ny, nz, rows, cap), out_shap...]
    all_to_all x1 -> x0, blocking collectives: 20.2 us -> none  [body(): lax.all_to_all(request, 'space', split_axis=1, concat_axis=1, tiled=True)]
    ppermute x4 -> x0, starting transfers between devices: 16.3 us -> none  [the longest x2 8.51 us: extended(): lax.ppermute(lax.slice_in_dim(block, block.shape[dim] - width, None, axis...]
    all_gather x1 -> x0, blocking collectives: 13.5 us -> none  [body(): whole = lax.all_gather(template, 'subj', axis=1, tiled=True)]
    slice x15 -> x0, local copies, waits for them, and re-layouts: 11.5 us -> none  [the longest x2 4.28 us: shift_down(): body_part = lax.slice_in_dim(field, 0, field.shape[axis] - 1, axis=axis)]
    sub x2 -> x0, other arithmetic: 8.33 us -> none  [body(): field = field - smooth_z(rowwise)]
    div x4 -> x0, other arithmetic: 7.28 us -> none  [the longest x2 4.6 us: body(): (predicted - current[None]) / (grads[0] * grads[0] + grads[1] * grads[1]...]
  transfers between devices with their start and end apart: 7 -> 0, of which waited for: 5 -> 0; matrix products, arithmetic and copies ran while one was open for 2% -> 0% of each run, Pallas kernels for 0% -> 0%
where the time goes in v1:
time: 127 us; the launch traced here: 125 us
  Pallas kernels  120 us (94%)
  local copies, waits for them, and re-layouts  4.61 us (4%)
    pallas_call x1, Pallas kernels, body(): pl.pallas_call(functools.partial(kernel, nj, ny, nz, rows, cap), out_shap...  120 us
    unnamed x4, local copies, waits for them, and re-layouts  4.61 us

profile of v1, /device:TPU:8, one launch (start us, length us, event | category | flops | bytes accessed | tf_op | source)
XLA Modules:
  0.0 125.3 jit_solution(15822639800218502593)
XLA Ops:
  0.6 120.1 %demons.1 = (f32[3,2,64,16,128]{4,3,2,1,0:T(8,128)}, f32[128,128]{1,0:T(8,128)}) custom-call(bf16[2,64,16,128]{3,2,1,0:T(8,128)(2,1)} %img_h.1, f32[3,2,64,16,128]{4,3,2,1,0:T(8,128)} %vel_h.1, bf16[3,2,64,16,128]{4,3,2,1,0:T(8,128)(2,1)} %wts_h.1, f32[128,128]{1,0:T(8,128)} %bitcast.6, s32[2,1,64]{2,1,0:T(1,128)} %bitcast.8, s32[2,64]{1,0:T(2,128)} %loc_ref.1, ...), custom_call_target="tpu_custom_call" | custom-call | tf_op jit(solution)/shard_map/demons/pallas_call | solution.py:559
  120.7 0.0 copy-start
  120.7 4.0 %copy.12 = f32[3,2,64,16,128]{4,3,2,1,0:T(8,128)} copy(f32[3,2,64,16,128]{4,3,2,1,0:T(8,128)} %get-tuple-element.8) | data formatting | bytes 6291456
  124.7 0.0 copy-done
  124.7 0.6 copy.13
Async XLA Ops:
  120.7 4.0 %copy-start = (f32[128,128]{1,0:T(8,128)S(1)}, f32[128,128]{1,0:T(8,128)}, u32[]{:S(2)}) copy-start(f32[128,128]{1,0:T(8,128)} %get-tuple-element.5) | copy-start | bytes 196612

commit v2 on v1

--- a/solution.py
+++ b/solution.py
@@ -17,11 +17,11 @@
 def kernel(
     nj, ny, nz, rows, cap,
     img_h, vel_h, wts_h, tin_ref, own_ref, loc_ref, cnt_ref,
-    out_h, tout_ref,
-    img, wts, f, sendb, recvb0, recvb1, warp, g, q, r, pr, cur0, cur1, total,
-    tsend, trecv, req, rreq, slot_v, rreq_s, slot_s, edge, halo,
+    f, tout_ref,
+    img, wts, sendb, recvb0, recvb1, warp, g, q, r, pr, cur0, cur1, total,
+    tsend, trecv, req, req_y, req_z, slot_v, rreq_s, slot_s, edge, halo,
     part, crecv, xsend, xrecv, fsend, frecv, fx, fxrecv,
-    in_sem, out_sem, tsend_sem, trecv_sem, qsend_sem, qrecv_sem, loc_sem,
+    in_sem, tsend_sem, trecv_sem, qsend_sem, qrecv_sem, loc_sem,
     bsend_sem, brecv_sem, hsend_sem, hrecv_sem,
     csend_sem, crecv_sem, xsend_sem, xrecv_sem, gsend_sem, grecv_sem,
     asend_sem, arecv_sem, fsend_sem, frecv_sem, ysend_sem, yrecv_sem,
@@ -35,6 +35,8 @@
     y, z = sp // nz, sp % nz
     mate = x * 2 + (1 - c)
     recvb = (recvb0, recvb1)
+    warp_step = 4
+    step = max(2, rows // 8)
     half = rows // 2
     piece = rows // nj
 
@@ -52,15 +54,21 @@
 
     barrier = pltpu.get_barrier_semaphore()
 
-    def greet(j, carry):
-        pl.semaphore_signal(barrier, inc=1, device_id=(sj, peer(j)), device_id_type=MESH)
-        return carry
+    def along_y(i):
+        return ((y + i) % ny) * nz + z
+
+    def along_z(i):
+        return y * nz + (z + i) % nz
+
+    for i in range(1, ny):
+        pl.semaphore_signal(barrier, inc=1, device_id=(sj, along_y(i)), device_id_type=MESH)
+    for i in range(1, nz):
+        pl.semaphore_signal(barrier, inc=1, device_id=(sj, along_z(i)), device_id_type=MESH)
 
     def greet_subj(i, carry):
         pl.semaphore_signal(barrier, inc=1, device_id=((sj + i) % nj, sp), device_id_type=MESH)
         return carry
 
-    lax.fori_loop(1, ns, greet, 0)
     lax.fori_loop(1, nj, greet_subj, 0)
 
     for p in range(pd):
@@ -91,34 +99,49 @@
             column = jnp.sum(jnp.where(mine, loc_ref[s : s + 1, :], 0), axis=1, keepdims=True)
             asked = asked + jnp.where(lane == s * cap + k, column, 0)
     for d in range(ns):
-        req[d] = asked[d : d + 1, :]
+        req[d // nz, d % nz] = asked[d : d + 1, :]
     slots_in = pltpu.make_async_copy(slot_v, slot_s, loc_sem.at[0])
     slots_in.start()
 
-    pl.semaphore_wait(barrier, ns - 1 + nj - 1)
-
-    def ask(j):
-        d = peer(j)
-        return pltpu.make_async_remote_copy(
-            src_ref=req.at[d], dst_ref=rreq.at[sp],
-            send_sem=qsend_sem.at[j], recv_sem=qrecv_sem.at[sp],
-            device_id=(sj, d), device_id_type=MESH,
-        )
-
-    def asked_by(d):
-        return pltpu.make_async_remote_copy(
-            src_ref=req.at[d], dst_ref=rreq.at[d],
-            send_sem=qsend_sem.at[0], recv_sem=qrecv_sem.at[d],
-            device_id=(sj, sp), device_id_type=MESH,
-        )
-
-    def start_ask(j, carry):
-        ask(j).start()
-        return carry
-
-    lax.fori_loop(1, ns, start_ask, 0)
-    own_ask = pltpu.make_async_copy(req.at[sp], rreq.at[sp], loc_sem.at[1])
-    own_ask.start()
+    pl.semaphore_wait(barrier, ny - 1 + nz - 1 + nj - 1)
+
+    def ask_y(i):
+        return pltpu.make_async_remote_copy(
+            src_ref=req.at[(y + i) % ny], dst_ref=req_y.at[y],
+            send_sem=qsend_sem.at[0, i], recv_sem=qrecv_sem.at[0, y],
+            device_id=(sj, along_y(i)), device_id_type=MESH,
+        )
+
+    def asked_y(i):
+        return pltpu.make_async_remote_copy(
+            src_ref=req.at[0], dst_ref=req_y.at[(y + i) % ny],
+            send_sem=qsend_sem.at[0, i], recv_sem=qrecv_sem.at[0, (y + i) % ny],
+            device_id=(sj, sp), device_id_type=MESH,
+        )
+
+    def ask_z(i):
+        return pltpu.make_async_remote_copy(
+            src_ref=req_y.at[:, (z + i) % nz], dst_ref=req_z.at[z],
+            send_sem=qsend_sem.at[1, i], recv_sem=qrecv_sem.at[1, z],
+            device_id=(sj, along_z(i)), device_id_type=MESH,
+        )
+
+    def asked_z(i):
+        return pltpu.make_async_remote_copy(
+            src_ref=req_y.at[:, 0], dst_ref=req_z.at[(z + i) % nz],
+            send_sem=qsend_sem.at[1, i], recv_sem=qrecv_sem.at[1, (z + i) % nz],
+            device_id=(sj, sp), device_id_type=MESH,
+        )
+
+    for i in range(1, ny):
+        ask_y(i).start()
+    req_y[y] = req[y]
+    for i in range(1, ny):
+        asked_y(i).wait_recv()
+    for i in range(1, nz):
+        ask_z(i).start()
+    for n in range(ny):
+        req_z[z, n] = req_y[n, z]
 
     def plane_copy(i):
         return pltpu.make_async_remote_copy(
@@ -133,13 +156,9 @@
 
     lax.fori_loop(1, nj, start_planes, 0)
 
-    def wait_ask(j, carry):
-        asked_by(peer(j)).wait_recv()
-        return carry
-
-    own_ask.wait()
-    lax.fori_loop(1, ns, wait_ask, 0)
-    rreq_in = pltpu.make_async_copy(rreq, rreq_s, loc_sem.at[2])
+    for i in range(1, nz):
+        asked_z(i).wait_recv()
+    rreq_in = pltpu.make_async_copy(req_z, rreq_s, loc_sem.at[2])
     rreq_in.start()
     img_in.wait()
     rreq_in.wait()
@@ -164,7 +183,7 @@
         def gather(j, carry):
             d = peer(j)
             for k in range(cap):
-                sendb[s, d * cap + k] = img[s, rreq_s[d, 0, s * cap + k]]
+                sendb[s, d * cap + k] = img[s, rreq_s[d % nz, d // nz, 0, s * cap + k]]
 
             @pl.when(j >= 2)
             def _():
@@ -174,7 +193,7 @@
 
         lax.fori_loop(1, ns, gather, 0)
         for k in range(cap):
-            recvb[s][sp * cap + k] = img[s, rreq_s[sp, 0, s * cap + k]]
+            recvb[s][sp * cap + k] = img[s, rreq_s[z, y, 0, s * cap + k]]
         brick(s, ns - 1).start()
 
     def wait_planes(i, carry):
@@ -248,7 +267,7 @@
         first = count // 2
         last = rows - (count - first)
 
-        def warp_tile(t, carry):
+        def warp_tile(t):
             b00 = pair_of(recvb[s][slot_s[s, 0, t]].astype(F32))
             wx, wy, wz = [pair_of(wts[a, s, t].astype(F32)) for a in range(3)]
             live = jnp.where((t < first) | (t >= last), 1.0, 0.0).astype(F32)
@@ -287,9 +306,13 @@
             put(g, (2, s, t), gz)
             put(q, (s, t), qq)
             put(r, (s, t), rr)
+
+        def warp_block(b, carry):
+            for n in range(warp_step):
+                warp_tile(b * warp_step + n)
             return carry
 
-        lax.fori_loop(0, rows, warp_tile, 0)
+        lax.fori_loop(0, rows // warp_step, warp_block, 0)
 
     def first_ratio(s, t):
         return pair_of(r[s, t])
@@ -368,18 +391,26 @@
                 total[pl.ds(here, 8), :] = total[pl.ds(here, 8), :] + pred[0]
                 total[pl.ds(here + 8, 8), :] = total[pl.ds(here + 8, 8), :] + pred[1]
 
+        def add(p, o):
+            return [a + b for a, b in zip(p, o)]
+
+        def run(s, start, low_row, high_row):
+            u = update(s, start)
+            two = add(low_row or update(s, start - 1), u)
+            for n in range(step):
+                at_end = n == step - 1
+                after = high_row if at_end and high_row else update(s, start + n + 1)
+                ahead = add(u, after)
+                advance(s, start + n, add(two, ahead))
+                u, two = after, ahead
+
         for s in range(2):
-            u0, u1 = update(s, 0), update(s, 1)
-            before = [a + b for a, b in zip(u0, u1)]
-
-            def inner(t, carry):
-                before, u = list(carry[:6]), list(carry[6:])
-                after = update(s, t + 1)
-                two = [a + b for a, b in zip(u, after)]
-                advance(s, t, [a + b for a, b in zip(before, two)])
-                return tuple(two + after)
-
-            lax.fori_loop(1, rows - 1, inner, tuple(before + u1))
+
+            def inner(b, carry):
+                run(s, b * step, None, None)
+                return carry
+
+            lax.fori_loop(1, rows // step - 1, inner, 0)
 
         @pl.when(sp > 0)
         def _():
@@ -389,13 +420,15 @@
         def _():
             halo_in(it, 1).wait_recv()
 
+        def halo_row(side, s):
+            out = []
+            for a in range(3):
+                out += pair_of(halo[it, side, a, s])
+            return out
+
         for s in range(2):
-            for side, t, near in ((0, 0, 1), (1, rows - 1, rows - 2)):
-                u, v = update(s, t), update(s, near)
-                far = []
-                for a in range(3):
-                    far += pair_of(halo[it, side, a, s])
-                advance(s, t, [(far[n] + u[n]) + (u[n] + v[n]) for n in range(6)])
+            run(s, 0, halo_row(0, s), None)
+            run(s, rows - step, None, halo_row(1, s))
 
     iterate(0)
 
@@ -467,9 +500,6 @@
     to_mate.wait_send()
 
     iterate(1)
-
-    vel_out = pltpu.make_async_copy(f, out_h, out_sem.at[0])
-    vel_out.start()
 
     for cc in range(2):
         for xx in range(nx):
@@ -501,13 +531,17 @@
     for p in range(pd):
         tout_ref[pl.ds(p, rows, stride=pd), :] = acc[p] * scale
 
-    def sent_ask(j, carry):
-        ask(j).wait_send()
+    for i in range(1, ny):
+        ask_y(i).wait_send()
+    for i in range(1, nz):
+        ask_z(i).wait_send()
+
+    def sent_bricks(j, carry):
         brick(0, j).wait_send()
         brick(1, j).wait_send()
         return carry
 
-    lax.fori_loop(1, ns, sent_ask, 0)
+    lax.fori_loop(1, ns, sent_bricks, 0)
 
     def sent_planes(i, carry):
         plane_copy(i).wait_send()
@@ -539,7 +573,6 @@
             send_sem=ysend_sem.at[i], recv_sem=yrecv_sem.at[x],
             device_id=(chip(i) * 2 + c, sp), device_id_type=MESH,
         ).wait_send()
-    vel_out.wait()
 
 
 def body(nj, ny, nz, images, velocity, weights, template, owners, local_rows, tile_counts):
@@ -553,21 +586,20 @@
     piece = rows // nj * PLANE
     vmem = pl.BlockSpec(memory_space=pltpu.VMEM)
     smem = pl.BlockSpec(memory_space=pltpu.SMEM)
-    away = pl.BlockSpec(memory_space=pl.ANY)
+    away = pl.BlockSpec(memory_space=pltpu.HBM)
     bf16 = jnp.bfloat16
     dma = pltpu.SemaphoreType.DMA
     field, planes = pl.pallas_call(
         functools.partial(kernel, nj, ny, nz, rows, cap),
         out_shape=(
-            jax.ShapeDtypeStruct(velocity.shape, F32),
+            pltpu.VMEM(velocity.shape, F32),
             jax.ShapeDtypeStruct((rows * pd, LANES), F32),
         ),
         in_specs=[away, away, away, vmem, vmem, vmem, smem],
-        out_specs=(away, vmem),
+        out_specs=(vmem, vmem),
         scratch_shapes=[
             pltpu.VMEM((2, rows) + brick, bf16),
             pltpu.VMEM((3, 2, rows) + brick, bf16),
-            pltpu.VMEM((3, 2, rows) + brick, F32),
             pltpu.VMEM((2, slots) + brick, bf16),
             pltpu.VMEM((slots,) + brick, bf16),
             pltpu.VMEM((slots,) + brick, bf16),
@@ -581,10 +613,11 @@
             pltpu.VMEM((rows * PLANE, LANES), F32),
             pltpu.VMEM((pd, rows, LANES), F32),
             pltpu.VMEM((nj, pd, rows, LANES), F32),
-            pltpu.VMEM((ns, 1, LANES), I32),
-            pltpu.VMEM((ns, 1, LANES), I32),
+            pltpu.VMEM((ny, nz, 1, LANES), I32),
+            pltpu.VMEM((ny, nz, 1, LANES), I32),
+            pltpu.VMEM((nz, ny, 1, LANES), I32),
             pltpu.VMEM((2, 1, LANES), I32),
-            pltpu.SMEM((ns, 1, LANES), I32),
+            pltpu.SMEM((nz, ny, 1, LANES), I32),
             pltpu.SMEM((2, 1, LANES), I32),
             pltpu.VMEM((2, 2, 3, 2) + brick, F32),
             pltpu.VMEM((2, 2, 3, 2) + brick, F32),
@@ -596,13 +629,13 @@
             pltpu.VMEM((nx, pd, rows, LANES), F32),
             pltpu.VMEM((nx, pd, rows, LANES), F32),
             pltpu.VMEM((nx, pd, rows, LANES), F32),
-            dma((3,)), dma((1,)), dma((nj,)), dma((nj,)), dma((ns,)), dma((ns,)), dma((3,)),
+            dma((3,)), dma((nj,)), dma((nj,)), dma((2, nz)), dma((2, nz)), dma((4,)),
             dma((2, ns)), dma((2, ns)), dma((2, 2)), dma((2, 2)),
             dma((1,)), dma((1,)), dma((nx,)), dma((nx,)), dma((nx,)), dma((nx,)),
             dma((nx,)), dma((nx,)), dma((1,)), dma((1,)), dma((nx,)), dma((nx,)),
         ],
         compiler_params=pltpu.CompilerParams(
-            collective_id=0, has_side_effects=True, vmem_limit_bytes=56 * 1024 * 1024
+            collective_id=0, has_side_effects=True, vmem_limit_bytes=62200 * 1024
         ),
         name="demons",
     )(

time: 127 us -> 82.1 us (0.65)
  Pallas kernels: 120 us -> 78.1 us
  local copies, waits for them, and re-layouts: 4.61 us -> 2.3 us
    pallas_call x1, Pallas kernels: 120 us -> 78.1 us  [body(): pl.pallas_call(functools.partial(kernel, nj, ny, nz, rows, cap), out_shap...]
    unnamed x4, local copies, waits for them, and re-layouts: 4.61 us -> 2.3 us
where the time goes in v2:
time: 82.1 us; the launch traced here: 81 us
  Pallas kernels  78.1 us (95%)
  local copies, waits for them, and re-layouts  2.3 us (3%)
    pallas_call x1, Pallas kernels, body(): pl.pallas_call(functools.partial(kernel, nj, ny, nz, rows, cap), out_shap...  78.1 us
    unnamed x4, local copies, waits for them, and re-layouts  2.3 us

profile of v2, /device:TPU:8, one launch (start us, length us, event | category | flops | bytes accessed | tf_op | source)
XLA Modules:
  0.0 81.0 jit_solution(4956881336274311510)
XLA Ops:
  0.6 78.1 %demons.1 = (f32[3,2,64,16,128]{4,3,2,1,0:T(8,128)S(1)}, f32[128,128]{1,0:T(8,128)}) custom-call(bf16[2,64,16,128]{3,2,1,0:T(8,128)(2,1)} %img_h.1, f32[3,2,64,16,128]{4,3,2,1,0:T(8,128)} %vel_h.1, bf16[3,2,64,16,128]{4,3,2,1,0:T(8,128)(2,1)} %wts_h.1, f32[128,128]{1,0:T(8,128)} %bitcast.6, s32[2,1,64]{2,1,0:T(1,128)} %bitcast.8, s32[2,64]{1,0:T(2,128)} %loc_ref.1, ...), custom_call_target="tpu_custom_call" | custom-call | tf_op jit(solution)/shard_map/demons/pallas_call | solution.py:592
  78.7 0.0 copy-start
  78.7 1.7 %copy.12 = f32[3,2,64,16,128]{4,3,2,1,0:T(8,128)} copy(f32[3,2,64,16,128]{4,3,2,1,0:T(8,128)S(1)} %get-tuple-element.6) | data formatting | bytes 6291456
  80.4 0.0 copy-done
  80.4 0.6 copy.13
Async XLA Ops:
  78.7 1.7 %copy-start = (f32[128,128]{1,0:T(8,128)S(1)}, f32[128,128]{1,0:T(8,128)}, u32[]{:S(2)}) copy-start(f32[128,128]{1,0:T(8,128)} %get-tuple-element.5) | copy-start | bytes 196612

commit v3 on v2

--- a/solution.py
+++ b/solution.py
@@ -35,10 +35,8 @@
     y, z = sp // nz, sp % nz
     mate = x * 2 + (1 - c)
     recvb = (recvb0, recvb1)
-    warp_step = 4
+    warp_step = 4 if rows >= 32 else 2
     step = max(2, rows // 8)
-    half = rows // 2
-    piece = rows // nj
 
     def peer(j):
         dy, zi = j % ny, j // ny
@@ -256,13 +254,14 @@
 
     both = (0, 1)
 
-    for s in range(2):
-
+    def arrivals(s):
         def arrived(j, carry):
             brick_from(s, peer(j)).wait_recv()
             return carry
 
         lax.fori_loop(1, ns, arrived, 0)
+
+    def warp_blocks(s, start, stop):
         count = cnt_ref[0, s]
         first = count // 2
         last = rows - (count - first)
@@ -312,7 +311,7 @@
                 warp_tile(b * warp_step + n)
             return carry
 
-        lax.fori_loop(0, rows // warp_step, warp_block, 0)
+        lax.fori_loop(start, stop, warp_block, 0)
 
     def first_ratio(s, t):
         return pair_of(r[s, t])
@@ -324,212 +323,292 @@
         qq = pair_of(q[s, t])
         return [(p1[i] - now[i]) * qq[i] for i in both]
 
-    def edge_copy(it, side):
+    def edge_copy(it, side, s):
         d = sp - 1 if side == 0 else sp + 1
         return pltpu.make_async_remote_copy(
-            src_ref=edge.at[it, side], dst_ref=halo.at[it, 1 - side],
-            send_sem=hsend_sem.at[it, side], recv_sem=hrecv_sem.at[it, 1 - side],
+            src_ref=edge.at[it, side, s], dst_ref=halo.at[it, 1 - side, s],
+            send_sem=hsend_sem.at[it, side, s], recv_sem=hrecv_sem.at[it, 1 - side, s],
             device_id=(sj, d), device_id_type=MESH,
         )
 
-    def halo_in(it, side):
-        return pltpu.make_async_remote_copy(
-            src_ref=edge.at[it, side], dst_ref=halo.at[it, side],
-            send_sem=hsend_sem.at[it, side], recv_sem=hrecv_sem.at[it, side],
+    def halo_in(it, side, s):
+        return pltpu.make_async_remote_copy(
+            src_ref=edge.at[it, side, s], dst_ref=halo.at[it, side, s],
+            send_sem=hsend_sem.at[it, side, s], recv_sem=hrecv_sem.at[it, side, s],
             device_id=(sj, sp), device_id_type=MESH,
         )
 
-    def iterate(it):
-        ratio = first_ratio if it == 0 else second_ratio
-
-        def update(s, t):
-            rr = ratio(s, t)
+    def inside(side):
+        return sp > 0 if side == 0 else sp < ns - 1
+
+    def update(it, s, t):
+        rr = first_ratio(s, t) if it == 0 else second_ratio(s, t)
+        out = []
+        for a in range(3):
+            gg = pair_of(g[a, s, t])
+            out += [gg[0] * rr[0], gg[1] * rr[1]]
+        return out
+
+    def send_edge(it, side, s):
+        u = update(it, s, 0 if side == 0 else rows - 1)
+        for a in range(3):
+            put(edge, (it, side, s, a), u[2 * a : 2 * a + 2])
+
+        @pl.when(inside(side))
+        def _():
+            edge_copy(it, side, s).start()
+
+    def wait_halo(it, side, s):
+        @pl.when(inside(side))
+        def _():
+            halo_in(it, side, s).wait_recv()
+
+    def advance(it, s, t, v):
+        new = []
+        for a in range(3):
+            old = pair_of(f[a, s, t])
             out = []
-            for a in range(3):
-                gg = pair_of(g[a, s, t])
-                out += [gg[0] * rr[0], gg[1] * rr[1]]
-            return out
-
-        for s in range(2):
-            for side, t in ((0, 0), (1, rows - 1)):
-                u = update(s, t)
-                for a in range(3):
-                    put(edge, (it, side, a, s), u[2 * a : 2 * a + 2])
-
-        @pl.when(sp > 0)
-        def _():
-            edge_copy(it, 0).start()
-
-        @pl.when(sp < ns - 1)
-        def _():
-            edge_copy(it, 1).start()
-
-        def advance(s, t, v):
-            new = []
-            for a in range(3):
-                old = pair_of(f[a, s, t])
-                out = []
-                for i in both:
-                    value = v[2 * a + i]
-                    two = value + down_z(value)
-                    out.append(old[i] - (two + jnp.where(z_top, value, pltpu.roll(two, LANES - 1, 1))))
-                put(f, (a, s, t), out)
-                new.append(out)
-            w = pair_of(warp[s, t])
-            gg = [pair_of(g[a, s, t]) for a in range(3)]
-            pred = [
-                w[i] + (gg[0][i] * new[0][i] + gg[1][i] * new[1][i]) + gg[2][i] * new[2][i]
-                for i in both
-            ]
-            if it == 0:
-                put(pr, (s, t), pred)
-            here = pl.multiple_of(t * PLANE, PLANE)
-            if s == 0:
-                total[pl.ds(here, 8), :] = pred[0]
-                total[pl.ds(here + 8, 8), :] = pred[1]
-            else:
-                total[pl.ds(here, 8), :] = total[pl.ds(here, 8), :] + pred[0]
-                total[pl.ds(here + 8, 8), :] = total[pl.ds(here + 8, 8), :] + pred[1]
-
-        def add(p, o):
-            return [a + b for a, b in zip(p, o)]
-
-        def run(s, start, low_row, high_row):
-            u = update(s, start)
-            two = add(low_row or update(s, start - 1), u)
-            for n in range(step):
-                at_end = n == step - 1
-                after = high_row if at_end and high_row else update(s, start + n + 1)
-                ahead = add(u, after)
-                advance(s, start + n, add(two, ahead))
-                u, two = after, ahead
-
-        for s in range(2):
-
-            def inner(b, carry):
-                run(s, b * step, None, None)
-                return carry
-
-            lax.fori_loop(1, rows // step - 1, inner, 0)
-
-        @pl.when(sp > 0)
-        def _():
-            halo_in(it, 0).wait_recv()
-
-        @pl.when(sp < ns - 1)
-        def _():
-            halo_in(it, 1).wait_recv()
-
-        def halo_row(side, s):
-            out = []
-            for a in range(3):
-                out += pair_of(halo[it, side, a, s])
-            return out
-
-        for s in range(2):
-            run(s, 0, halo_row(0, s), None)
-            run(s, rows - step, None, halo_row(1, s))
-
-    iterate(0)
-
-    mine = c * half * PLANE
-    other = (1 - c) * half * PLANE
-    span = half * PLANE
-    block = piece * PLANE
-
-    to_mate = pltpu.make_async_remote_copy(
-        src_ref=total.at[pl.ds(other, span)], dst_ref=crecv,
-        send_sem=csend_sem.at[0], recv_sem=crecv_sem.at[0],
-        device_id=(mate, sp), device_id_type=MESH,
-    )
-    to_mate.start()
-    to_mate.wait_recv()
-    xsend[...] = total[pl.ds(mine, span), :] + crecv[...]
+            for i in both:
+                value = v[2 * a + i]
+                two = value + down_z(value)
+                out.append(old[i] - (two + jnp.where(z_top, value, pltpu.roll(two, LANES - 1, 1))))
+            put(f, (a, s, t), out)
+            new.append(out)
+        w = pair_of(warp[s, t])
+        gg = [pair_of(g[a, s, t]) for a in range(3)]
+        pred = [
+            w[i] + (gg[0][i] * new[0][i] + gg[1][i] * new[1][i]) + gg[2][i] * new[2][i]
+            for i in both
+        ]
+        if it == 0:
+            put(pr, (s, t), pred)
+        here = pl.multiple_of(t * PLANE, PLANE)
+        if s == 0:
+            total[pl.ds(here, 8), :] = pred[0]
+            total[pl.ds(here + 8, 8), :] = pred[1]
+        else:
+            total[pl.ds(here, 8), :] = total[pl.ds(here, 8), :] + pred[0]
+            total[pl.ds(here + 8, 8), :] = total[pl.ds(here + 8, 8), :] + pred[1]
+
+    def add(p, o):
+        return [a + b for a, b in zip(p, o)]
+
+    def run(it, s, start, low_row, high_row):
+        u = update(it, s, start)
+        two = add(low_row or update(it, s, start - 1), u)
+        for n in range(step):
+            at_end = n == step - 1
+            after = high_row if at_end and high_row else update(it, s, start + n + 1)
+            ahead = add(u, after)
+            advance(it, s, start + n, add(two, ahead))
+            u, two = after, ahead
+
+    def smooth(it, s, start, stop):
+        def inner(b, carry):
+            run(it, s, b * step, None, None)
+            return carry
+
+        lax.fori_loop(start, stop, inner, 0)
+
+    def smooth_edge(it, side, s):
+        far = []
+        for a in range(3):
+            far += pair_of(halo[it, side, s, a])
+        if side == 0:
+            run(it, s, 0, far, None)
+        else:
+            run(it, s, rows - step, None, far)
 
     def chip(i):
         return (x + i) % nx
 
-    for i in range(1, nx):
-        pltpu.make_async_remote_copy(
-            src_ref=xsend.at[pl.ds(chip(i) * block, block)], dst_ref=xrecv.at[x],
-            send_sem=xsend_sem.at[i], recv_sem=xrecv_sem.at[x],
+    quarter = rows // 4 * PLANE
+    block = rows // (2 * nj) * PLANE
+    scale = 1.0 / (2.0 * nj)
+
+    def mine(k):
+        return (2 * k + c) * quarter
+
+    def other(k):
+        return (2 * k + 1 - c) * quarter
+
+    def to_mate(k):
+        return pltpu.make_async_remote_copy(
+            src_ref=total.at[pl.ds(other(k), quarter)], dst_ref=crecv.at[k],
+            send_sem=csend_sem.at[k], recv_sem=crecv_sem.at[k],
+            device_id=(mate, sp), device_id_type=MESH,
+        )
+
+    def across(k, i):
+        return pltpu.make_async_remote_copy(
+            src_ref=xsend.at[k, pl.ds(chip(i) * block, block)], dst_ref=xrecv.at[k, x],
+            send_sem=xsend_sem.at[k, i], recv_sem=xrecv_sem.at[k, x],
             device_id=(chip(i) * 2 + c, sp), device_id_type=MESH,
-        ).start()
-    acc = xsend[pl.ds(x * block, block), :]
-    for i in range(1, nx):
-        pltpu.make_async_remote_copy(
-            src_ref=xrecv.at[0], dst_ref=xrecv.at[chip(i)],
-            send_sem=xsend_sem.at[i], recv_sem=xrecv_sem.at[chip(i)],
-            device_id=(sj, sp), device_id_type=MESH,
-        ).wait_recv()
-        acc = acc + xrecv[chip(i)]
-    scale = 1.0 / (2.0 * nj)
-    home = mine + x * block
-    part[...] = acc * scale
-
-    def spread(i):
-        return pltpu.make_async_remote_copy(
-            src_ref=part, dst_ref=cur1.at[pl.ds(home, block)],
-            send_sem=gsend_sem.at[i], recv_sem=grecv_sem.at[x],
+        )
+
+    def spread(k, i):
+        return pltpu.make_async_remote_copy(
+            src_ref=part.at[k], dst_ref=cur1.at[pl.ds(mine(k) + x * block, block)],
+            send_sem=gsend_sem.at[k, i], recv_sem=grecv_sem.at[k, x],
             device_id=(chip(i) * 2 + c, sp), device_id_type=MESH,
         )
 
-    def spread_mate(src, where, n):
-        return pltpu.make_async_remote_copy(
-            src_ref=src, dst_ref=cur1.at[pl.ds(where, block)],
-            send_sem=asend_sem.at[n], recv_sem=arecv_sem.at[n],
+    def spread_mate(k, i):
+        where = mine(k) + chip(i) * block
+        return pltpu.make_async_remote_copy(
+            src_ref=part.at[k] if i == 0 else cur1.at[pl.ds(where, block)],
+            dst_ref=cur1.at[pl.ds(where, block)],
+            send_sem=asend_sem.at[k, i], recv_sem=arecv_sem.at[k, i],
             device_id=(mate, sp), device_id_type=MESH,
         )
 
-    for i in range(1, nx):
-        spread(i).start()
-    spread_mate(part, home, 0).start()
-    cur1[pl.ds(home, block), :] = acc * scale
-    for i in range(1, nx):
-        where = mine + chip(i) * block
-        pltpu.make_async_remote_copy(
-            src_ref=part, dst_ref=cur1.at[pl.ds(where, block)],
-            send_sem=gsend_sem.at[i], recv_sem=grecv_sem.at[chip(i)],
-            device_id=(sj, sp), device_id_type=MESH,
-        ).wait_recv()
-        spread_mate(cur1.at[pl.ds(where, block)], where, i).start()
-    for i in range(nx):
-        where = other + chip(i) * block
-        spread_mate(part, where, i).wait_recv()
-
-    to_mate.wait_send()
-
-    iterate(1)
-
-    for cc in range(2):
-        for xx in range(nx):
+    def mean_pair(k):
+        to_mate(k).wait_recv()
+        xsend[k] = total[pl.ds(mine(k), quarter), :] + crecv[k]
+        for i in range(1, nx):
+            across(k, i).start()
+
+    def mean_sum(k):
+        acc = xsend[k, pl.ds(x * block, block), :]
+        for i in range(1, nx):
+            pltpu.make_async_remote_copy(
+                src_ref=part.at[k], dst_ref=xrecv.at[k, chip(i)],
+                send_sem=xsend_sem.at[k, i], recv_sem=xrecv_sem.at[k, chip(i)],
+                device_id=(sj, sp), device_id_type=MESH,
+            ).wait_recv()
+            acc = acc + xrecv[k, chip(i)]
+        part[k] = acc * scale
+        for i in range(1, nx):
+            spread(k, i).start()
+        spread_mate(k, 0).start()
+        cur1[pl.ds(mine(k) + x * block, block), :] = acc * scale
+
+    def mean_pass(k):
+        for i in range(1, nx):
+            where = mine(k) + chip(i) * block
+            pltpu.make_async_remote_copy(
+                src_ref=part.at[k], dst_ref=cur1.at[pl.ds(where, block)],
+                send_sem=gsend_sem.at[k, i], recv_sem=grecv_sem.at[k, chip(i)],
+                device_id=(sj, sp), device_id_type=MESH,
+            ).wait_recv()
+            spread_mate(k, i).start()
+
+    def mean_done(k):
+        for i in range(nx):
+            where = other(k) + chip(i) * block
+            pltpu.make_async_remote_copy(
+                src_ref=part.at[k], dst_ref=cur1.at[pl.ds(where, block)],
+                send_sem=asend_sem.at[k, i], recv_sem=arecv_sem.at[k, i],
+                device_id=(sj, sp), device_id_type=MESH,
+            ).wait_recv()
+
+    nb = rows // step
+    nw = rows // warp_step
+    mid = nb // 2
+
+    arrivals(0)
+    warp_blocks(0, 0, nw)
+    send_edge(0, 0, 0)
+    send_edge(0, 1, 0)
+    smooth(0, 0, 1, nb - 1)
+    arrivals(1)
+    warp_blocks(1, nw - 1, nw)
+    warp_blocks(1, 0, 1)
+    send_edge(0, 0, 1)
+    send_edge(0, 1, 1)
+    warp_blocks(1, 1, nw - 1)
+    smooth(0, 1, 1, mid)
+    for s in range(2):
+        wait_halo(0, 0, s)
+        smooth_edge(0, 0, s)
+    to_mate(0).start()
+    smooth(0, 1, mid, nb - 1)
+    for s in range(2):
+        wait_halo(0, 1, s)
+        smooth_edge(0, 1, s)
+    to_mate(1).start()
+    for k in range(2):
+        mean_pair(k)
+    for k in range(2):
+        mean_sum(k)
+    for k in range(2):
+        mean_pass(k)
+    for k in range(2):
+        to_mate(k).wait_send()
+
+    mean_done(0)
+    for s in range(2):
+        send_edge(1, 0, s)
+    for s in range(2):
+        smooth(1, s, 1, mid - 1)
+    mean_done(1)
+    for s in range(2):
+        send_edge(1, 1, s)
+    for s in range(2):
+        smooth(1, s, mid - 1, nb - 1)
+
+    def sort_planes(b):
+        base = b * step * PLANE
+        for cc in range(2):
+            for xx in range(nx):
+                for p in range(pd):
+                    plane = (2 * xx + cc) * pd + p
+                    fsend[b, cc, xx, p] = total[pl.ds(base + plane, step, stride=PLANE), :]
+
+    inner_blocks, ends = pl.ds(1, nb - 2), (pl.ds(0, 1), pl.ds(nb - 1, 1))
+    pieces = (inner_blocks,) + ends
+
+    def planes_to_mate(n):
+        return pltpu.make_async_remote_copy(
+            src_ref=fsend.at[pieces[n], 1 - c], dst_ref=frecv.at[pieces[n]],
+            send_sem=fsend_sem.at[n], recv_sem=frecv_sem.at[n],
+            device_id=(mate, sp), device_id_type=MESH,
+        )
+
+    def planes_across(n, i):
+        return pltpu.make_async_remote_copy(
+            src_ref=fx.at[chip(i), pieces[n]], dst_ref=fxrecv.at[x, pieces[n]],
+            send_sem=ysend_sem.at[n, i], recv_sem=yrecv_sem.at[n, x],
+            device_id=(chip(i) * 2 + c, sp), device_id_type=MESH,
+        )
+
+    def planes_pair(n, blocks):
+        planes_to_mate(n).wait_recv()
+        for b in blocks:
+            for xx in range(nx):
+                fx[xx, b] = fsend[b, c, xx] + frecv[b, xx]
+        for i in range(1, nx):
+            planes_across(n, i).start()
+
+    def planes_sum(n, blocks):
+        for i in range(1, nx):
+            pltpu.make_async_remote_copy(
+                src_ref=fxrecv.at[0, pieces[n]], dst_ref=fxrecv.at[chip(i), pieces[n]],
+                send_sem=ysend_sem.at[n, i], recv_sem=yrecv_sem.at[n, chip(i)],
+                device_id=(sj, sp), device_id_type=MESH,
+            ).wait_recv()
+        for b in blocks:
+            acc = fx[x, b]
+            for i in range(1, nx):
+                acc = acc + fxrecv[chip(i), b]
             for p in range(pd):
-                plane = (2 * xx + cc) * pd + p
-                fsend[cc, xx, p] = total[pl.ds(plane, rows, stride=PLANE), :]
-    planes_to_mate = pltpu.make_async_remote_copy(
-        src_ref=fsend.at[1 - c], dst_ref=frecv,
-        send_sem=fsend_sem.at[0], recv_sem=frecv_sem.at[0],
-        device_id=(mate, sp), device_id_type=MESH,
-    )
-    planes_to_mate.start()
-    planes_to_mate.wait_recv()
-    fx[...] = fsend[c] + frecv[...]
-    for i in range(1, nx):
-        pltpu.make_async_remote_copy(
-            src_ref=fx.at[chip(i)], dst_ref=fxrecv.at[x],
-            send_sem=ysend_sem.at[i], recv_sem=yrecv_sem.at[x],
-            device_id=(chip(i) * 2 + c, sp), device_id_type=MESH,
-        ).start()
-    acc = fx[x]
-    for i in range(1, nx):
-        pltpu.make_async_remote_copy(
-            src_ref=fxrecv.at[0], dst_ref=fxrecv.at[chip(i)],
-            send_sem=ysend_sem.at[i], recv_sem=yrecv_sem.at[chip(i)],
-            device_id=(sj, sp), device_id_type=MESH,
-        ).wait_recv()
-        acc = acc + fxrecv[chip(i)]
-    for p in range(pd):
-        tout_ref[pl.ds(p, rows, stride=pd), :] = acc[p] * scale
+                tout_ref[pl.ds(b * step * pd + p, step, stride=pd), :] = acc[p] * scale
+
+    for b in range(1, nb - 1):
+        sort_planes(b)
+    planes_to_mate(0).start()
+    for side in range(2):
+        for s in range(2):
+            wait_halo(1, side, s)
+            smooth_edge(1, side, s)
+        sort_planes(0 if side == 0 else nb - 1)
+        planes_to_mate(1 + side).start()
+    planes_pair(0, range(1, nb - 1))
+    planes_pair(1, (0,))
+    planes_pair(2, (nb - 1,))
+    planes_sum(0, range(1, nb - 1))
+    planes_sum(1, (0,))
+    planes_sum(2, (nb - 1,))
 
     for i in range(1, ny):
         ask_y(i).wait_send()
@@ -548,31 +627,24 @@
         return carry
 
     lax.fori_loop(1, nj, sent_planes, 0)
-    for it in range(2):
-
-        @pl.when(sp > 0)
+    for side in range(2):
+
+        @pl.when(inside(side))
         def _():
-            edge_copy(it, 0).wait_send()
-
-        @pl.when(sp < ns - 1)
-        def _():
-            edge_copy(it, 1).wait_send()
-
-    planes_to_mate.wait_send()
-    for i in range(nx):
-        spread_mate(part, home, i).wait_send()
-    for i in range(1, nx):
-        spread(i).wait_send()
-        pltpu.make_async_remote_copy(
-            src_ref=xsend.at[pl.ds(chip(i) * block, block)], dst_ref=xrecv.at[x],
-            send_sem=xsend_sem.at[i], recv_sem=xrecv_sem.at[x],
-            device_id=(chip(i) * 2 + c, sp), device_id_type=MESH,
-        ).wait_send()
-        pltpu.make_async_remote_copy(
-            src_ref=fx.at[chip(i)], dst_ref=fxrecv.at[x],
-            send_sem=ysend_sem.at[i], recv_sem=yrecv_sem.at[x],
-            device_id=(chip(i) * 2 + c, sp), device_id_type=MESH,
-        ).wait_send()
+            for it in range(2):
+                for s in range(2):
+                    edge_copy(it, side, s).wait_send()
+
+    for k in range(2):
+        for i in range(nx):
+            spread_mate(k, i).wait_send()
+        for i in range(1, nx):
+            across(k, i).wait_send()
+            spread(k, i).wait_send()
+    for n in range(3):
+        planes_to_mate(n).wait_send()
+        for i in range(1, nx):
+            planes_across(n, i).wait_send()
 
 
 def body(nj, ny, nz, images, velocity, weights, template, owners, local_rows, tile_counts):
@@ -583,7 +655,9 @@
     cap = 2 * rows // ns
     slots = ns * cap
     brick = (PLANE, LANES)
-    piece = rows // nj * PLANE
+    piece = rows // (2 * nj) * PLANE
+    step = max(2, rows // 8)
+    nb = rows // step
     vmem = pl.BlockSpec(memory_space=pltpu.VMEM)
     smem = pl.BlockSpec(memory_space=pltpu.SMEM)
     away = pl.BlockSpec(memory_space=pltpu.HBM)
@@ -619,20 +693,20 @@
             pltpu.VMEM((2, 1, LANES), I32),
             pltpu.SMEM((nz, ny, 1, LANES), I32),
             pltpu.SMEM((2, 1, LANES), I32),
-            pltpu.VMEM((2, 2, 3, 2) + brick, F32),
-            pltpu.VMEM((2, 2, 3, 2) + brick, F32),
-            pltpu.VMEM((piece, LANES), F32),
-            pltpu.VMEM((rows // 2 * PLANE, LANES), F32),
-            pltpu.VMEM((rows // 2 * PLANE, LANES), F32),
-            pltpu.VMEM((nx, piece, LANES), F32),
-            pltpu.VMEM((2, nx, pd, rows, LANES), F32),
-            pltpu.VMEM((nx, pd, rows, LANES), F32),
-            pltpu.VMEM((nx, pd, rows, LANES), F32),
-            pltpu.VMEM((nx, pd, rows, LANES), F32),
+            pltpu.VMEM((2, 2, 2, 3) + brick, F32),
+            pltpu.VMEM((2, 2, 2, 3) + brick, F32),
+            pltpu.VMEM((2, piece, LANES), F32),
+            pltpu.VMEM((2, rows // 4 * PLANE, LANES), F32),
+            pltpu.VMEM((2, rows // 4 * PLANE, LANES), F32),
+            pltpu.VMEM((2, nx, piece, LANES), F32),
+            pltpu.VMEM((nb, 2, nx, pd, step, LANES), F32),
+            pltpu.VMEM((nb, nx, pd, step, LANES), F32),
+            pltpu.VMEM((nx, nb, pd, step, LANES), F32),
+            pltpu.VMEM((nx, nb, pd, step, LANES), F32),
             dma((3,)), dma((nj,)), dma((nj,)), dma((2, nz)), dma((2, nz)), dma((4,)),
-            dma((2, ns)), dma((2, ns)), dma((2, 2)), dma((2, 2)),
-            dma((1,)), dma((1,)), dma((nx,)), dma((nx,)), dma((nx,)), dma((nx,)),
-            dma((nx,)), dma((nx,)), dma((1,)), dma((1,)), dma((nx,)), dma((nx,)),
+            dma((2, ns)), dma((2, ns)), dma((2, 2, 2)), dma((2, 2, 2)),
+            dma((2,)), dma((2,)), dma((2, nx)), dma((2, nx)), dma((2, nx)), dma((2, nx)),
+            dma((2, nx)), dma((2, nx)), dma((3,)), dma((3,)), dma((3, nx)), dma((3, nx)),
         ],
         compiler_params=pltpu.CompilerParams(
             collective_id=0, has_side_effects=True, vmem_limit_bytes=62200 * 1024

time: 82.1 us -> 76.7 us (0.934)
  Pallas kernels: 78.1 us -> 73.4 us
    pallas_call x1, Pallas kernels: 78.1 us -> 73.4 us  [body(): pl.pallas_call(functools.partial(kernel, nj, ny, nz, rows, cap), out_shap...]
where the time goes in v3:
time: 76.7 us; the launch traced here: 76.3 us
  Pallas kernels  73.4 us (96%)
  local copies, waits for them, and re-layouts  2.3 us (3%)
    pallas_call x1, Pallas kernels, body(): pl.pallas_call(functools.partial(kernel, nj, ny, nz, rows, cap), out_shap...  73.4 us
    unnamed x4, local copies, waits for them, and re-layouts  2.3 us

profile of v3, /device:TPU:8, one launch (start us, length us, event | category | flops | bytes accessed | tf_op | source)
XLA Modules:
  0.0 76.3 jit_solution(2075947471234975453)
XLA Ops:
  0.6 73.4 %demons.1 = (f32[3,2,64,16,128]{4,3,2,1,0:T(8,128)S(1)}, f32[128,128]{1,0:T(8,128)}) custom-call(bf16[2,64,16,128]{3,2,1,0:T(8,128)(2,1)} %img_h.1, f32[3,2,64,16,128]{4,3,2,1,0:T(8,128)} %vel_h.1, bf16[3,2,64,16,128]{4,3,2,1,0:T(8,128)(2,1)} %wts_h.1, f32[128,128]{1,0:T(8,128)} %bitcast.6, s32[2,1,64]{2,1,0:T(1,128)} %bitcast.8, s32[2,64]{1,0:T(2,128)} %loc_ref.1, ...), custom_call_target="tpu_custom_call" | custom-call | tf_op jit(solution)/shard_map/demons/pallas_call | solution.py:666
  74.0 0.0 copy-start
  74.0 1.7 %copy.12 = f32[3,2,64,16,128]{4,3,2,1,0:T(8,128)} copy(f32[3,2,64,16,128]{4,3,2,1,0:T(8,128)S(1)} %get-tuple-element.6) | data formatting | bytes 6291456
  75.7 0.0 copy-done
  75.7 0.6 copy.13
Async XLA Ops:
  74.0 1.7 %copy-start = (f32[128,128]{1,0:T(8,128)S(1)}, f32[128,128]{1,0:T(8,128)}, u32[]{:S(2)}) copy-start(f32[128,128]{1,0:T(8,128)} %get-tuple-element.5) | copy-start | bytes 196612

commit v4 on v3

--- a/solution.py
+++ b/solution.py
@@ -18,11 +18,11 @@
     nj, ny, nz, rows, cap,
     img_h, vel_h, wts_h, tin_ref, own_ref, loc_ref, cnt_ref,
     f, tout_ref,
-    img, wts, sendb, recvb0, recvb1, warp, g, q, r, pr, cur0, cur1, total,
+    img, below0, below1, above0, above1, wts, sendb, recvb0, recvb1, warp, g, q, r, pr, cur0, cur1, total,
     tsend, trecv, req, req_y, req_z, slot_v, rreq_s, slot_s, edge, halo,
     part, crecv, xsend, xrecv, fsend, frecv, fx, fxrecv,
     in_sem, tsend_sem, trecv_sem, qsend_sem, qrecv_sem, loc_sem,
-    bsend_sem, brecv_sem, hsend_sem, hrecv_sem,
+    lsend_sem, lrecv_sem, bsend_sem, brecv_sem, hsend_sem, hrecv_sem,
     csend_sem, crecv_sem, xsend_sem, xrecv_sem, gsend_sem, grecv_sem,
     asend_sem, arecv_sem, fsend_sem, frecv_sem, ysend_sem, yrecv_sem,
 ):
@@ -38,10 +38,13 @@
     warp_step = 4 if rows >= 32 else 2
     step = max(2, rows // 8)
 
-    def peer(j):
-        dy, zi = j % ny, j // ny
-        dz = jnp.where(zi % 2 == 1, (zi + 1) // 2, nz - zi // 2)
-        return ((y + dy) % ny) * nz + (z + dz) % nz
+    every, even, odd = (0, ny, 1), (0, ny, 2), (1, ny, 2)
+    serves = (
+        (0, 0, every), (0, -1, every), (0, 1, every),
+        (1, -1, every), (2, -1, every), (3, -1, even),
+        (-1, 1, every), (-2, 1, every), (-3, 1, odd),
+    )
+    order = (5, 8, 1, 4, 7, 2, 3, 6, 0)
 
     img_in = pltpu.make_async_copy(img_h, img, in_sem.at[0])
     img_in.start()
@@ -56,12 +59,12 @@
         return ((y + i) % ny) * nz + z
 
     def along_z(i):
-        return y * nz + (z + i) % nz
+        return y * nz + (z + nz + i) % nz
 
     for i in range(1, ny):
         pl.semaphore_signal(barrier, inc=1, device_id=(sj, along_y(i)), device_id_type=MESH)
-    for i in range(1, nz):
-        pl.semaphore_signal(barrier, inc=1, device_id=(sj, along_z(i)), device_id_type=MESH)
+    for e in range(3, 9):
+        pl.semaphore_signal(barrier, inc=1, device_id=(sj, along_z(serves[e][0])), device_id_type=MESH)
 
     def greet_subj(i, carry):
         pl.semaphore_signal(barrier, inc=1, device_id=((sj + i) % nj, sp), device_id_type=MESH)
@@ -101,7 +104,7 @@
     slots_in = pltpu.make_async_copy(slot_v, slot_s, loc_sem.at[0])
     slots_in.start()
 
-    pl.semaphore_wait(barrier, ny - 1 + nz - 1 + nj - 1)
+    pl.semaphore_wait(barrier, ny - 1 + 6 + nj - 1)
 
     def ask_y(i):
         return pltpu.make_async_remote_copy(
@@ -117,29 +120,52 @@
             device_id=(sj, sp), device_id_type=MESH,
         )
 
-    def ask_z(i):
-        return pltpu.make_async_remote_copy(
-            src_ref=req_y.at[:, (z + i) % nz], dst_ref=req_z.at[z],
-            send_sem=qsend_sem.at[1, i], recv_sem=qrecv_sem.at[1, z],
-            device_id=(sj, along_z(i)), device_id_type=MESH,
-        )
-
-    def asked_z(i):
-        return pltpu.make_async_remote_copy(
-            src_ref=req_y.at[:, 0], dst_ref=req_z.at[(z + i) % nz],
-            send_sem=qsend_sem.at[1, i], recv_sem=qrecv_sem.at[1, (z + i) % nz],
+    def ask_z(e):
+        back, image, _ = serves[e]
+        return pltpu.make_async_remote_copy(
+            src_ref=req_y.at[:, (z + nz - back + image) % nz], dst_ref=req_z.at[e],
+            send_sem=qsend_sem.at[1, e], recv_sem=qrecv_sem.at[1, e],
+            device_id=(sj, along_z(-back)), device_id_type=MESH,
+        )
+
+    def asked_z(e):
+        return pltpu.make_async_remote_copy(
+            src_ref=req_y.at[:, 0], dst_ref=req_z.at[e],
+            send_sem=qsend_sem.at[1, e], recv_sem=qrecv_sem.at[1, e],
+            device_id=(sj, sp), device_id_type=MESH,
+        )
+
+    below, above = (below0, below1), (above0, above1)
+
+    def lend(s, side):
+        return pltpu.make_async_remote_copy(
+            src_ref=img.at[s], dst_ref=below[s] if side == 0 else above[s],
+            send_sem=lsend_sem.at[s, side], recv_sem=lrecv_sem.at[s, side],
+            device_id=(sj, along_z(1 if side == 0 else -1)), device_id_type=MESH,
+        )
+
+    def lent(s, side):
+        return pltpu.make_async_remote_copy(
+            src_ref=img.at[s], dst_ref=below[s] if side == 0 else above[s],
+            send_sem=lsend_sem.at[s, side], recv_sem=lrecv_sem.at[s, side],
             device_id=(sj, sp), device_id_type=MESH,
         )
 
     for i in range(1, ny):
         ask_y(i).start()
+    img_in.wait()
+    lend(0, 0).start()
+    lend(0, 1).start()
     req_y[y] = req[y]
     for i in range(1, ny):
         asked_y(i).wait_recv()
-    for i in range(1, nz):
-        ask_z(i).start()
-    for n in range(ny):
-        req_z[z, n] = req_y[n, z]
+    for e in (5, 8, 4, 7, 3, 6):
+        ask_z(e).start()
+    lend(1, 0).start()
+    lend(1, 1).start()
+    for e in range(3):
+        for n in range(ny):
+            req_z[e, n] = req_y[n, (z + nz + serves[e][1]) % nz]
 
     def plane_copy(i):
         return pltpu.make_async_remote_copy(
@@ -154,45 +180,67 @@
 
     lax.fori_loop(1, nj, start_planes, 0)
 
-    for i in range(1, nz):
-        asked_z(i).wait_recv()
+    for e in range(3, 9):
+        asked_z(e).wait_recv()
     rreq_in = pltpu.make_async_copy(req_z, rreq_s, loc_sem.at[2])
     rreq_in.start()
-    img_in.wait()
     rreq_in.wait()
 
-    def brick(s, j):
-        d = peer(j)
-        return pltpu.make_async_remote_copy(
-            src_ref=sendb.at[s, pl.ds(d * cap, cap)], dst_ref=recvb[s].at[pl.ds(sp * cap, cap)],
-            send_sem=bsend_sem.at[s, j], recv_sem=brecv_sem.at[s, sp],
+    def owner_of(e):
+        return y * nz + (z + nz + serves[e][1]) % nz
+
+    def brick(s, e, dy):
+        d = ((y + dy) % ny) * nz + (z + nz + serves[e][0]) % nz
+        return pltpu.make_async_remote_copy(
+            src_ref=sendb.at[s, pl.ds((e * ny + dy) * cap, cap)],
+            dst_ref=recvb[s].at[pl.ds(owner_of(e) * cap, cap)],
+            send_sem=bsend_sem.at[s, e * ny + dy], recv_sem=brecv_sem.at[s, owner_of(e)],
             device_id=(sj, d), device_id_type=MESH,
         )
 
     def brick_from(s, d):
         return pltpu.make_async_remote_copy(
-            src_ref=sendb.at[s, pl.ds(d * cap, cap)], dst_ref=recvb[s].at[pl.ds(d * cap, cap)],
+            src_ref=sendb.at[s, pl.ds(0, cap)], dst_ref=recvb[s].at[pl.ds(d * cap, cap)],
             send_sem=bsend_sem.at[s, 0], recv_sem=brecv_sem.at[s, d],
             device_id=(sj, sp), device_id_type=MESH,
         )
 
-    for s in range(2):
-
-        def gather(j, carry):
-            d = peer(j)
+    def over_y(e, what):
+        first, last, stride = serves[e][2]
+        first = first + stride if serves[e][0] == 0 else first
+        count = len(range(first, last, stride))
+
+        def one(i, carry):
+            what(first + i * stride)
+            return carry
+
+        if count:
+            lax.fori_loop(0, count, one, 0)
+
+    def wanted(s, e, dy, k):
+        where = rreq_s[e, (y + dy) % ny, 0, s * cap + k]
+        if serves[e][1] == 0:
+            return img[s, where]
+        return below[s][where] if serves[e][1] < 0 else above[s][where]
+
+    for s in range(2):
+        lent(s, 0).wait_recv()
+        lent(s, 1).wait_recv()
+        started = None
+        for e in order:
+
+            def gather(dy, s=s, e=e):
+                for k in range(cap):
+                    sendb[s, (e * ny + dy) * cap + k] = wanted(s, e, dy, k)
+
+            over_y(e, gather)
+            if started is not None:
+                over_y(started, lambda dy, s=s, e=started: brick(s, e, dy).start())
+            started = e
+        for e in range(3):
             for k in range(cap):
-                sendb[s, d * cap + k] = img[s, rreq_s[d % nz, d // nz, 0, s * cap + k]]
-
-            @pl.when(j >= 2)
-            def _():
-                brick(s, j - 1).start()
-
-            return carry
-
-        lax.fori_loop(1, ns, gather, 0)
-        for k in range(cap):
-            recvb[s][sp * cap + k] = img[s, rreq_s[z, y, 0, s * cap + k]]
-        brick(s, ns - 1).start()
+                recvb[s][owner_of(e) * cap + k] = wanted(s, e, 0, k)
+        over_y(started, lambda dy, s=s, e=started: brick(s, e, dy).start())
 
     def wait_planes(i, carry):
         other = (sj + i) % nj
@@ -255,11 +303,16 @@
     both = (0, 1)
 
     def arrivals(s):
-        def arrived(j, carry):
-            brick_from(s, peer(j)).wait_recv()
+        def far(n, carry):
+            brick_from(s, ((y + 1 + n // nz) % ny) * nz + n % nz).wait_recv()
             return carry
 
-        lax.fori_loop(1, ns, arrived, 0)
+        def near(n, carry):
+            brick_from(s, y * nz + (z + n) % nz).wait_recv()
+            return carry
+
+        lax.fori_loop(0, (ny - 1) * nz, far, 0)
+        lax.fori_loop(2, nz - 1, near, 0)
 
     def warp_blocks(s, start, stop):
         count = cnt_ref[0, s]
@@ -612,15 +665,13 @@
 
     for i in range(1, ny):
         ask_y(i).wait_send()
-    for i in range(1, nz):
-        ask_z(i).wait_send()
-
-    def sent_bricks(j, carry):
-        brick(0, j).wait_send()
-        brick(1, j).wait_send()
-        return carry
-
-    lax.fori_loop(1, ns, sent_bricks, 0)
+    for e in range(3, 9):
+        ask_z(e).wait_send()
+    for s in range(2):
+        lend(s, 0).wait_send()
+        lend(s, 1).wait_send()
+        for e in order:
+            over_y(e, lambda dy, s=s, e=e: brick(s, e, dy).wait_send())
 
     def sent_planes(i, carry):
         plane_copy(i).wait_send()
@@ -673,8 +724,12 @@
         out_specs=(vmem, vmem),
         scratch_shapes=[
             pltpu.VMEM((2, rows) + brick, bf16),
+            pltpu.VMEM((rows,) + brick, bf16),
+            pltpu.VMEM((rows,) + brick, bf16),
+            pltpu.VMEM((rows,) + brick, bf16),
+            pltpu.VMEM((rows,) + brick, bf16),
             pltpu.VMEM((3, 2, rows) + brick, bf16),
-            pltpu.VMEM((2, slots) + brick, bf16),
+            pltpu.VMEM((2, 9 * ny * cap) + brick, bf16),
             pltpu.VMEM((slots,) + brick, bf16),
             pltpu.VMEM((slots,) + brick, bf16),
             pltpu.VMEM((2, rows) + brick, F32),
@@ -689,9 +744,9 @@
             pltpu.VMEM((nj, pd, rows, LANES), F32),
             pltpu.VMEM((ny, nz, 1, LANES), I32),
             pltpu.VMEM((ny, nz, 1, LANES), I32),
-            pltpu.VMEM((nz, ny, 1, LANES), I32),
+            pltpu.VMEM((9, ny, 1, LANES), I32),
             pltpu.VMEM((2, 1, LANES), I32),
-            pltpu.SMEM((nz, ny, 1, LANES), I32),
+            pltpu.SMEM((9, ny, 1, LANES), I32),
             pltpu.SMEM((2, 1, LANES), I32),
             pltpu.VMEM((2, 2, 2, 3) + brick, F32),
             pltpu.VMEM((2, 2, 2, 3) + brick, F32),
@@ -703,8 +758,8 @@
             pltpu.VMEM((nb, nx, pd, step, LANES), F32),
             pltpu.VMEM((nx, nb, pd, step, LANES), F32),
             pltpu.VMEM((nx, nb, pd, step, LANES), F32),
-            dma((3,)), dma((nj,)), dma((nj,)), dma((2, nz)), dma((2, nz)), dma((4,)),
-            dma((2, ns)), dma((2, ns)), dma((2, 2, 2)), dma((2, 2, 2)),
+            dma((3,)), dma((nj,)), dma((nj,)), dma((2, 9)), dma((2, 9)), dma((4,)),
+            dma((2, 2)), dma((2, 2)), dma((2, 9 * ny)), dma((2, ns)), dma((2, 2, 2)), dma((2, 2, 2)),
             dma((2,)), dma((2,)), dma((2, nx)), dma((2, nx)), dma((2, nx)), dma((2, nx)),
             dma((2, nx)), dma((2, nx)), dma((3,)), dma((3,)), dma((3, nx)), dma((3, nx)),
         ],

time: 76.7 us -> 71.3 us (0.930)
  Pallas kernels: 73.4 us -> 68.2 us
    pallas_call x1, Pallas kernels: 73.4 us -> 68.2 us  [body(): pl.pallas_call(functools.partial(kernel, nj, ny, nz, rows, cap), out_shap...]
where the time goes in v4:
time: 71.3 us; the launch traced here: 71.2 us
  Pallas kernels  68.2 us (96%)
  local copies, waits for them, and re-layouts  2.3 us (3%)
    pallas_call x1, Pallas kernels, body(): pl.pallas_call(functools.partial(kernel, nj, ny, nz, rows, cap), out_shap...  68.2 us
    unnamed x4, local copies, waits for them, and re-layouts  2.3 us

profile of v4, /device:TPU:8, one launch (start us, length us, event | category | flops | bytes accessed | tf_op | source)
XLA Modules:
  0.0 71.2 jit_solution(5444665790463450911)
XLA Ops:
  0.6 68.2 %demons.1 = (f32[3,2,64,16,128]{4,3,2,1,0:T(8,128)S(1)}, f32[128,128]{1,0:T(8,128)}) custom-call(bf16[2,64,16,128]{3,2,1,0:T(8,128)(2,1)} %img_h.1, f32[3,2,64,16,128]{4,3,2,1,0:T(8,128)} %vel_h.1, bf16[3,2,64,16,128]{4,3,2,1,0:T(8,128)(2,1)} %wts_h.1, f32[128,128]{1,0:T(8,128)} %bitcast.6, s32[2,1,64]{2,1,0:T(1,128)} %bitcast.8, s32[2,64]{1,0:T(2,128)} %loc_ref.1, ...), custom_call_target="tpu_custom_call" | custom-call | tf_op jit(solution)/shard_map/demons/pallas_call | solution.py:717
  68.9 0.0 copy-start
  68.9 1.7 %copy.12 = f32[3,2,64,16,128]{4,3,2,1,0:T(8,128)} copy(f32[3,2,64,16,128]{4,3,2,1,0:T(8,128)S(1)} %get-tuple-element.6) | data formatting | bytes 6291456
  70.6 0.0 copy-done
  70.6 0.6 copy.13
Async XLA Ops:
  68.9 1.7 %copy-start = (f32[128,128]{1,0:T(8,128)S(1)}, f32[128,128]{1,0:T(8,128)}, u32[]{:S(2)}) copy-start(f32[128,128]{1,0:T(8,128)} %get-tuple-element.5) | copy-start | bytes 196612

commit v5 on v4

--- a/solution.py
+++ b/solution.py
@@ -35,7 +35,7 @@
     y, z = sp // nz, sp % nz
     mate = x * 2 + (1 - c)
     recvb = (recvb0, recvb1)
-    warp_step = 4 if rows >= 32 else 2
+    warp_step = 8 if rows >= 32 else 2
     step = max(2, rows // 8)
 
     every, even, odd = (0, ny, 1), (0, ny, 2), (1, ny, 2)
@@ -44,7 +44,7 @@
         (1, -1, every), (2, -1, every), (3, -1, even),
         (-1, 1, every), (-2, 1, every), (-3, 1, odd),
     )
-    order = (5, 8, 1, 4, 7, 2, 3, 6, 0)
+    order = ((1, 2, 0, 5, 8, 4, 7, 3, 6), (5, 8, 4, 7, 3, 6, 1, 2, 0))
 
     img_in = pltpu.make_async_copy(img_h, img, in_sem.at[0])
     img_in.start()
@@ -227,7 +227,7 @@
         lent(s, 0).wait_recv()
         lent(s, 1).wait_recv()
         started = None
-        for e in order:
+        for e in order[s]:
 
             def gather(dy, s=s, e=e):
                 for k in range(cap):
@@ -576,12 +576,12 @@
         smooth_edge(0, 0, s)
     to_mate(0).start()
     smooth(0, 1, mid, nb - 1)
+    mean_pair(0)
     for s in range(2):
         wait_halo(0, 1, s)
         smooth_edge(0, 1, s)
     to_mate(1).start()
-    for k in range(2):
-        mean_pair(k)
+    mean_pair(1)
     for k in range(2):
         mean_sum(k)
     for k in range(2):
@@ -656,7 +656,8 @@
             smooth_edge(1, side, s)
         sort_planes(0 if side == 0 else nb - 1)
         planes_to_mate(1 + side).start()
-    planes_pair(0, range(1, nb - 1))
+        if side == 0:
+            planes_pair(0, range(1, nb - 1))
     planes_pair(1, (0,))
     planes_pair(2, (nb - 1,))
     planes_sum(0, range(1, nb - 1))
@@ -670,7 +671,7 @@
     for s in range(2):
         lend(s, 0).wait_send()
         lend(s, 1).wait_send()
-        for e in order:
+        for e in order[s]:
             over_y(e, lambda dy, s=s, e=e: brick(s, e, dy).wait_send())
 
     def sent_planes(i, carry):

time: 71.3 us -> 69.7 us (0.978)
  Pallas kernels: 68.2 us -> 66.6 us
    pallas_call x1, Pallas kernels: 68.2 us -> 66.6 us  [body(): pl.pallas_call(functools.partial(kernel, nj, ny, nz, rows, cap), out_shap...]
where the time goes in v5:
time: 69.7 us; the launch traced here: 69.5 us
  Pallas kernels  66.6 us (96%)
  local copies, waits for them, and re-layouts  2.3 us (3%)
    pallas_call x1, Pallas kernels, body(): pl.pallas_call(functools.partial(kernel, nj, ny, nz, rows, cap), out_shap...  66.6 us
    unnamed x4, local copies, waits for them, and re-layouts  2.3 us

profile of v5, /device:TPU:8, one launch (start us, length us, event | category | flops | bytes accessed | tf_op | source)
XLA Modules:
  0.0 69.5 jit_solution(18403837455925980694)
XLA Ops:
  0.6 66.6 %demons.1 = (f32[3,2,64,16,128]{4,3,2,1,0:T(8,128)S(1)}, f32[128,128]{1,0:T(8,128)}) custom-call(bf16[2,64,16,128]{3,2,1,0:T(8,128)(2,1)} %img_h.1, f32[3,2,64,16,128]{4,3,2,1,0:T(8,128)} %vel_h.1, bf16[3,2,64,16,128]{4,3,2,1,0:T(8,128)(2,1)} %wts_h.1, f32[128,128]{1,0:T(8,128)} %bitcast.6, s32[2,1,64]{2,1,0:T(1,128)} %bitcast.8, s32[2,64]{1,0:T(2,128)} %loc_ref.1, ...), custom_call_target="tpu_custom_call" | custom-call | tf_op jit(solution)/shard_map/demons/pallas_call | solution.py:718
  67.2 0.0 copy-start
  67.2 1.7 %copy.12 = f32[3,2,64,16,128]{4,3,2,1,0:T(8,128)} copy(f32[3,2,64,16,128]{4,3,2,1,0:T(8,128)S(1)} %get-tuple-element.6) | data formatting | bytes 6291456
  68.9 0.0 copy-done
  68.9 0.6 copy.13
Async XLA Ops:
  67.2 1.7 %copy-start = (f32[128,128]{1,0:T(8,128)S(1)}, f32[128,128]{1,0:T(8,128)}, u32[]{:S(2)}) copy-start(f32[128,128]{1,0:T(8,128)} %get-tuple-element.5) | copy-start | bytes 196612

commit v6 on v5

--- a/solution.py
+++ b/solution.py
@@ -719,7 +719,7 @@
         functools.partial(kernel, nj, ny, nz, rows, cap),
         out_shape=(
             pltpu.VMEM(velocity.shape, F32),
-            jax.ShapeDtypeStruct((rows * pd, LANES), F32),
+            pltpu.VMEM((rows * pd, LANES), F32),
         ),
         in_specs=[away, away, away, vmem, vmem, vmem, smem],
         out_specs=(vmem, vmem),

time: 69.7 us -> 69 us (0.990)
    unnamed x4 -> x2, local copies, waits for them, and re-layouts: 2.3 us -> 2.3 us
where the time goes in v6:
time: 69 us; the launch traced here: 68.9 us
  Pallas kernels  66 us (96%)
  local copies, waits for them, and re-layouts  2.3 us (3%)
    pallas_call x1, Pallas kernels, body(): pl.pallas_call(functools.partial(kernel, nj, ny, nz, rows, cap), out_shap...  66 us
    unnamed x2, local copies, waits for them, and re-layouts  2.3 us

profile of v6, /device:TPU:8, one launch (start us, length us, event | category | flops | bytes accessed | tf_op | source)
XLA Modules:
  0.0 68.9 jit_solution(9170786325547949751)
XLA Ops:
  0.6 66.0 %demons.1 = (f32[3,2,64,16,128]{4,3,2,1,0:T(8,128)S(1)}, f32[128,128]{1,0:T(8,128)S(1)}) custom-call(bf16[2,64,16,128]{3,2,1,0:T(8,128)(2,1)} %img_h.1, f32[3,2,64,16,128]{4,3,2,1,0:T(8,128)} %vel_h.1, bf16[3,2,64,16,128]{4,3,2,1,0:T(8,128)(2,1)} %wts_h.1, f32[128,128]{1,0:T(8,128)} %bitcast.7, s32[2,1,64]{2,1,0:T(1,128)} %bitcast.8, s32[2,64]{1,0:T(2,128)} %loc_ref.1, ...), custom_call_target="tpu_custom_call" | custom-call | tf_op jit(solution)/shard_map/demons/pallas_call | solution.py:718
  66.6 1.7 %copy.12 = f32[3,2,64,16,128]{4,3,2,1,0:T(8,128)} copy(f32[3,2,64,16,128]{4,3,2,1,0:T(8,128)S(1)} %get-tuple-element.6) | data formatting | bytes 6291456
  68.3 0.6 copy.13
